TPU v7x, 512 devices: a whole 4x8x8 slice. The times are simulated.
512 devices in a mesh: tm: 32 (over y, x), state: 16 (over z, core).
Axes of the slice: x: 4, y: 8, z: 8, core: 2. Of those that a mesh axis runs over, the one named last changes fastest.
Arguments:
- prior: float32 [1024], replicated, may hold values from -6 to 6
- transition: bfloat16 [1024, 1024], replicated, may hold values from -1 to 1, as said below
- gain: bfloat16 [1024, 1024], replicated, may hold values from -1 to 1, as said below
- smoother: bfloat16 [1024, 1024], P('state'), may hold values from -1 to 1, as said below
- observed: float32 [128, 1024], P('tm'), may hold values from -6 to 6
- present: int32 [128], P('tm'), may hold values 0 or 1
Outputs:
- filtered: float32 [128, 1024], P('tm', 'state')
- smoothed: float32 [128, 1024], P('tm', 'state')
Inputs may be any that keep to these rules, and one draw needn't show every extreme that they name: transition: diagonal entries 1 - r with r log-uniform between 0.003 and 0.1 over the coefficients, plus an antisymmetric part whose entries have standard deviation about 0.1 / (2 sqrt(2048)) times sqrt(2). gain: diagonal entries log-uniform between 0.005 and 0.5, plus a symmetric part whose entries have standard deviation about 0.004 sqrt(2) / sqrt(1024). smoother: diagonal entries 1 - r with r log-uniform between 0.006 and 0.4, plus a symmetric part whose entries have standard deviation about 0.003 sqrt(2) / sqrt(1024); its spectral radius is below one.
All inputs are finite; a program needn't handle non-finite values. No bound on the sum of `present` on one device may be relied on, other than what follows from the above.
Results may differ from a plain program's by a relative error of at most 0.0003.
Values may be sent and summed in bfloat16 or wider, within the bound.
A program may use at most 128 MiB of HBM per device.

v0:
```python
import jax
import jax.numpy as jnp
from jax import lax
from jax.sharding import PartitionSpec as P

HIGH_PRECISION = lax.Precision.HIGHEST


def passed_along(block, axis, distance):
    devices = range(lax.axis_size(axis))
    route = [(i - distance, i) for i in devices if i - distance in devices]
    return lax.ppermute(block, axis, route)


def matvec(matrix, vector):
    return jnp.dot(matrix, vector, precision=HIGH_PRECISION, preferred_element_type=jnp.float32)


def assemble(panel_vector):
    return lax.all_gather(panel_vector, "state", axis=0, tiled=True)


def move_vector(vector, step_distance):
    return passed_along(vector, "tm", step_distance)


def local(prior, transition, gain, smoother, observed, present):
    step_count = observed.shape[0]
    panel_count = smoother.shape[0]
    width = transition.shape[0]
    device_count = lax.axis_size("tm")
    time_position = lax.axis_index("tm")
    first_row = lax.axis_index("state") * panel_count
    weights = present.astype(jnp.float32)
    is_first = time_position == 0
    is_final = time_position == device_count - 1

    def filter_step(state_vector, index):
        predicted = matvec(transition, state_vector)
        return predicted + weights[index] * matvec(gain, observed[index] - predicted)

    local_vector = jnp.where(is_first, prior, jnp.zeros_like(prior))
    for index in range(step_count):
        local_vector = filter_step(local_vector, index)
    column_numbers = lax.broadcasted_iota(jnp.int32, (panel_count, width), 1)
    row_ids = lax.broadcasted_iota(jnp.int32, (panel_count, width), 0) + first_row
    composite = (column_numbers == row_ids).astype(jnp.float32)
    for index in reversed(range(step_count)):
        reduced = lax.cond(
            present[index] > 0,
            lambda rows_now: rows_now
            - jnp.dot(rows_now, gain, precision=HIGH_PRECISION, preferred_element_type=jnp.float32),
            lambda rows_now: rows_now,
            composite,
        )
        composite = jnp.dot(
            reduced, transition, precision=HIGH_PRECISION, preferred_element_type=jnp.float32
        )
    composite = jnp.where(is_first, jnp.zeros_like(composite), composite)
    level_total = (device_count - 1).bit_length()
    reach = 4
    running = local_vector
    covered = 1
    for level_index in range(level_total):
        offset = 1 << level_index
        if offset < reach and 2 * offset < device_count:
            earlier_vector, earlier_rows = passed_along((running, composite), "tm", offset)
            current = composite
            product_rows = jnp.dot(
                current,
                lax.all_gather(earlier_rows, "state", axis=0, tiled=True),
                precision=HIGH_PRECISION,
                preferred_element_type=jnp.float32,
            )
            running = running + assemble(matvec(current, earlier_vector))
            composite = product_rows
            covered = 2 * offset
        else:
            relayed = running
            for repeat in range(offset // covered):
                relayed = move_vector(relayed, covered)
                relayed = assemble(matvec(composite, relayed))
            running = running + relayed
    entering = move_vector(running, 1)
    state_vector = jnp.where(is_first, prior, entering)
    state_list = []
    for index in range(step_count):
        state_vector = filter_step(state_vector, index)
        state_list.append(state_vector)
    state_list[-1] = running
    filtered_full = jnp.stack(state_list)
    smoother_matrix_full = lax.all_gather(smoother, "state", axis=0, tiled=True)
    predicted_state = jnp.einsum(
        "gf,yf->gy",
        filtered_full,
        transition,
        precision=HIGH_PRECISION,
        preferred_element_type=jnp.float32,
    )
    pulled = jnp.einsum(
        "gf,yf->gy",
        predicted_state,
        smoother_matrix_full,
        precision=HIGH_PRECISION,
        preferred_element_type=jnp.float32,
    )
    corrected = filtered_full - pulled
    last_row = (lax.broadcasted_iota(jnp.int32, (step_count, 1), 0) == step_count - 1) & is_final
    offsets = jnp.where(last_row, filtered_full, corrected)

    def smooth_step(next_vector, index):
        return matvec(smoother_matrix_full, next_vector) + offsets[index]

    suffix = jnp.zeros_like(prior)
    for index in reversed(range(step_count)):
        suffix = smooth_step(suffix, index)
    power_rows = smoother.astype(jnp.float32)
    for repeat in range(step_count - 1):
        power_rows = jnp.dot(
            power_rows,
            smoother_matrix_full,
            precision=HIGH_PRECISION,
            preferred_element_type=jnp.float32,
        )
    single_rows = power_rows
    for repeat in range(step_count):
        power_rows = jnp.dot(
            power_rows,
            smoother_matrix_full,
            precision=HIGH_PRECISION,
            preferred_element_type=jnp.float32,
        )
    gathered_total = suffix
    for level_index in range(level_total):
        offset = 1 << level_index
        later = move_vector(gathered_total, -offset)
        if offset == 1:
            later = assemble(matvec(single_rows, later))
        else:
            for repeat in range(offset // 2):
                later = assemble(matvec(power_rows, later))
        gathered_total = gathered_total + later
    next_vector = move_vector(gathered_total, -1)
    smooth_list = [None] * step_count
    for index in reversed(range(step_count)):
        next_vector = smooth_step(next_vector, index)
        smooth_list[index] = next_vector
    smoothed_full = jnp.stack(smooth_list)
    filtered_rows = lax.dynamic_slice_in_dim(filtered_full, first_row, panel_count, 1)
    smoothed_rows = lax.dynamic_slice_in_dim(smoothed_full, first_row, panel_count, 1)
    return (filtered_rows, smoothed_rows)


def solution(mesh):
    placed = (P(), P(), P(), P("state", None), P("tm", None), P("tm"))
    return jax.shard_map(
        local,
        mesh=mesh,
        in_specs=placed,
        out_specs=(P("tm", "state"), P("tm", "state")),
        check_vma=False,
    )
```

profile of v0, /device:TPU:1, one launch (start us, length us, event | category | flops | bytes accessed | tf_op | source)
XLA Modules:
  0.0 881.0 jit_solution(10190211686995073555)
XLA Ops:
  27.4 62.4 %all-gather.4.cloned.1.call-done = f32[1024,1024]{1,0:T(8,128)} async-done(((f32[64,1024]{1,0:T(8,128)}), f32[1024,1024]{1,0:T(8,128)}) %all-gather.4.cloned.1.call-update) | async-done | bytes 4194320 | tf_op jit(solution)/shard_map/all_gather | solution.py:71
  99.3 5.4 collective-permute-done.3
  128.0 25.4 %all-reduce = f32[1024]{0:T(1024)S(1)} all-reduce(f32[1024]{0:T(1024)S(1)} %dynamic-update-slice), channel_id=1, replica_groups=mesh['tm'=32,'state'=16] {'state'}, use_global_device_ids=true, to_apply=%add | all-reduce | flops 1024 | bytes 8192
  153.5 5.5 collective-permute-start.2
  160.2 25.4 %all-reduce.1 = f32[1024]{0:T(1024)S(1)} all-reduce(f32[1024]{0:T(1024)S(1)} %dynamic-update-slice.1), channel_id=1, replica_groups=mesh['tm'=32,'state'=16] {'state'}, use_global_device_ids=true, to_apply=%add.1 | all-reduce | flops 1024 | bytes 8192
  185.6 8.8 collective-permute-start.4
  199.8 23.7 %all-reduce.2 = f32[1024]{0:T(1024)S(1)} all-reduce(f32[1024]{0:T(1024)S(1)} %dynamic-update-slice.2), channel_id=1, replica_groups=mesh['tm'=32,'state'=16] {'state'}, use_global_device_ids=true, to_apply=%add.2 | all-reduce | flops 1024 | bytes 8192
  227.9 24.4 %all-reduce.3 = f32[1024]{0:T(1024)S(1)} all-reduce(f32[1024]{0:T(1024)S(1)} %dynamic-update-slice.3), channel_id=1, replica_groups=mesh['tm'=32,'state'=16] {'state'}, use_global_device_ids=true, to_apply=%add.3 | all-reduce | flops 1024 | bytes 8192
  258.8 23.8 %all-reduce.4 = f32[1024]{0:T(1024)S(1)} all-reduce(f32[1024]{0:T(1024)S(1)} %dynamic-update-slice.4), channel_id=1, replica_groups=mesh['tm'=32,'state'=16] {'state'}, use_global_device_ids=true, to_apply=%add.4 | all-reduce | flops 1024 | bytes 8192
  282.6 7.7 collective-permute-start.7
  293.6 23.8 %all-reduce.5 = f32[1024]{0:T(1024)S(1)} all-reduce(f32[1024]{0:T(1024)S(1)} %dynamic-update-slice.5), channel_id=1, replica_groups=mesh['tm'=32,'state'=16] {'state'}, use_global_device_ids=true, to_apply=%add.5 | all-reduce | flops 1024 | bytes 8192
  324.7 23.8 %all-reduce.6 = f32[1024]{0:T(1024)S(1)} all-reduce(f32[1024]{0:T(1024)S(1)} %dynamic-update-slice.6), channel_id=1, replica_groups=mesh['tm'=32,'state'=16] {'state'}, use_global_device_ids=true, to_apply=%add.6 | all-reduce | flops 1024 | bytes 8192
  354.9 23.8 %all-reduce.7 = f32[1024]{0:T(1024)S(1)} all-reduce(f32[1024]{0:T(1024)S(1)} %dynamic-update-slice.7), channel_id=1, replica_groups=mesh['tm'=32,'state'=16] {'state'}, use_global_device_ids=true, to_apply=%add.7 | all-reduce | flops 1024 | bytes 8192
  386.1 23.8 %all-reduce.8 = f32[1024]{0:T(1024)S(1)} all-reduce(f32[1024]{0:T(1024)S(1)} %dynamic-update-slice.8), channel_id=1, replica_groups=mesh['tm'=32,'state'=16] {'state'}, use_global_device_ids=true, to_apply=%add.8 | all-reduce | flops 1024 | bytes 8192
  441.0 24.7 %all-reduce.9 = f32[1024]{0:T(1024)S(1)} all-reduce(f32[1024]{0:T(1024)S(1)} %dynamic-update-slice.9), channel_id=1, replica_groups=mesh['tm'=32,'state'=16] {'state'}, use_global_device_ids=true, to_apply=%add.9 | all-reduce | flops 1024 | bytes 8192
  473.5 24.4 %all-reduce.10 = f32[1024]{0:T(1024)S(1)} all-reduce(f32[1024]{0:T(1024)S(1)} %dynamic-update-slice.10), channel_id=1, replica_groups=mesh['tm'=32,'state'=16] {'state'}, use_global_device_ids=true, to_apply=%add.10 | all-reduce | flops 1024 | bytes 8192
  499.2 4.9 collective-permute-done.14
  504.6 24.4 %all-reduce.11 = f32[1024]{0:T(1024)S(1)} all-reduce(f32[1024]{0:T(1024)S(1)} %dynamic-update-slice.11), channel_id=1, replica_groups=mesh['tm'=32,'state'=16] {'state'}, use_global_device_ids=true, to_apply=%add.11 | all-reduce | flops 1024 | bytes 8192
  529.5 23.5 %all-reduce.12 = f32[1024]{0:T(1024)S(1)} all-reduce(f32[1024]{0:T(1024)S(1)} %dynamic-update-slice.12), channel_id=1, replica_groups=mesh['tm'=32,'state'=16] {'state'}, use_global_device_ids=true, to_apply=%add.12 | all-reduce | flops 1024 | bytes 8192
  559.6 24.4 %all-reduce.13 = f32[1024]{0:T(1024)S(1)} all-reduce(f32[1024]{0:T(1024)S(1)} %dynamic-update-slice.13), channel_id=1, replica_groups=mesh['tm'=32,'state'=16] {'state'}, use_global_device_ids=true, to_apply=%add.13 | all-reduce | flops 1024 | bytes 8192
  584.5 23.5 %all-reduce.14 = f32[1024]{0:T(1024)S(1)} all-reduce(f32[1024]{0:T(1024)S(1)} %dynamic-update-slice.14), channel_id=1, replica_groups=mesh['tm'=32,'state'=16] {'state'}, use_global_device_ids=true, to_apply=%add.14 | all-reduce | flops 1024 | bytes 8192
  608.5 23.5 %all-reduce.15 = f32[1024]{0:T(1024)S(1)} all-reduce(f32[1024]{0:T(1024)S(1)} %dynamic-update-slice.15), channel_id=1, replica_groups=mesh['tm'=32,'state'=16] {'state'}, use_global_device_ids=true, to_apply=%add.15 | all-reduce | flops 1024 | bytes 8192
  632.6 23.5 %all-reduce.16 = f32[1024]{0:T(1024)S(1)} all-reduce(f32[1024]{0:T(1024)S(1)} %dynamic-update-slice.16), channel_id=1, replica_groups=mesh['tm'=32,'state'=16] {'state'}, use_global_device_ids=true, to_apply=%add.16 | all-reduce | flops 1024 | bytes 8192
  657.4 7.6 collective-permute-done.16
  665.6 24.4 %all-reduce.17 = f32[1024]{0:T(1024)S(1)} all-reduce(f32[1024]{0:T(1024)S(1)} %dynamic-update-slice.17), channel_id=1, replica_groups=mesh['tm'=32,'state'=16] {'state'}, use_global_device_ids=true, to_apply=%add.17 | all-reduce | flops 1024 | bytes 8192
  690.5 23.5 %all-reduce.18 = f32[1024]{0:T(1024)S(1)} all-reduce(f32[1024]{0:T(1024)S(1)} %dynamic-update-slice.18), channel_id=1, replica_groups=mesh['tm'=32,'state'=16] {'state'}, use_global_device_ids=true, to_apply=%add.18 | all-reduce | flops 1024 | bytes 8192
  714.5 23.5 %all-reduce.19 = f32[1024]{0:T(1024)S(1)} all-reduce(f32[1024]{0:T(1024)S(1)} %dynamic-update-slice.19), channel_id=1, replica_groups=mesh['tm'=32,'state'=16] {'state'}, use_global_device_ids=true, to_apply=%add.19 | all-reduce | flops 1024 | bytes 8192
  738.5 23.5 %all-reduce.20 = f32[1024]{0:T(1024)S(1)} all-reduce(f32[1024]{0:T(1024)S(1)} %dynamic-update-slice.20), channel_id=1, replica_groups=mesh['tm'=32,'state'=16] {'state'}, use_global_device_ids=true, to_apply=%add.20 | all-reduce | flops 1024 | bytes 8192
  762.6 23.5 %all-reduce.21 = f32[1024]{0:T(1024)S(1)} all-reduce(f32[1024]{0:T(1024)S(1)} %dynamic-update-slice.21), channel_id=1, replica_groups=mesh['tm'=32,'state'=16] {'state'}, use_global_device_ids=true, to_apply=%add.21 | all-reduce | flops 1024 | bytes 8192
  786.6 23.5 %all-reduce.22 = f32[1024]{0:T(1024)S(1)} all-reduce(f32[1024]{0:T(1024)S(1)} %dynamic-update-slice.22), channel_id=1, replica_groups=mesh['tm'=32,'state'=16] {'state'}, use_global_device_ids=true, to_apply=%add.22 | all-reduce | flops 1024 | bytes 8192
  810.6 23.5 %all-reduce.23 = f32[1024]{0:T(1024)S(1)} all-reduce(f32[1024]{0:T(1024)S(1)} %dynamic-update-slice.23), channel_id=1, replica_groups=mesh['tm'=32,'state'=16] {'state'}, use_global_device_ids=true, to_apply=%add.23 | all-reduce | flops 1024 | bytes 8192
  834.7 23.5 %all-reduce.24 = f32[1024]{0:T(1024)S(1)} all-reduce(f32[1024]{0:T(1024)S(1)} %dynamic-update-slice.24), channel_id=1, replica_groups=mesh['tm'=32,'state'=16] {'state'}, use_global_device_ids=true, to_apply=%add.24 | all-reduce | flops 1024 | bytes 8192
  (225 shorter events, 167.0 us)
Async XLA Ops:
  7.2 2.3 copy-start
  7.2 82.6 %all-gather.4.cloned.1.call-start = ((), (), s32[]{:S(2)}) async-start(), calls=%async_computation | async-start | bytes 4456448 | tf_op jit(solution)/shard_map/all_gather | solution.py:71
  22.0 4.6 collective-permute-start.1
  26.6 0.7 copy-start.7
  27.3 78.9 %copy-start.8 = (f32[1024]{0:T(1024)S(1)}, f32[1024]{0:T(1024)}, u32[]{:S(2)}) copy-start(f32[1024]{0:T(1024)} %param.14) | copy-start | bytes 12292
  27.3 167.1 %all-gather.6.cloned.1.call-start = ((), (), s32[]{:S(2)}) async-start(), calls=%async_computation.1 | async-start | bytes 4456448 | tf_op jit(solution)/shard_map/all_gather | solution.py:71
  94.6 13.3 %copy-start.9 = (f32[4,1024]{1,0:T(4,128)S(1)}, f32[4,1024]{1,0:T(4,128)}, u32[]{:S(2)}) copy-start(f32[4,1024]{1,0:T(4,128)} %param.18) | copy-start | bytes 49156
  94.6 13.3 %copy-start.10 = (s32[4]{0:T(128)S(1)}, s32[4]{0:T(128)}, u32[]{:S(2)}) copy-start(s32[4]{0:T(128)} %param.19) | copy-start | bytes 52
  94.7 10.0 %collective-permute-start.3 = (f32[64,1024]{1,0:T(8,128)S(1)}, f32[64,1024]{1,0:T(8,128)S(1)}, u32[]{:S(2)}, u32[]{:S(2)}) collective-permute-start(f32[64,1024]{1,0:T(8,128)S(1)} %fusion.24), channel_id=1, source_target_pairs={{0,32},{16,48},{32,64},{48,80},{64,96},{80,112},{96,128},{112,144}... | collective-permute-start | bytes 786440 | tf_op jit(solution)/shard_map/ppermute | solution.py:12
  104.7 0.7 copy-start.6
  105.4 150.7 %all-gather.8.cloned.1.call-start = ((), (), s32[]{:S(2)}) async-start(), calls=%async_computation.2 | async-start | bytes 2228224 | tf_op jit(solution)/shard_map/all_gather | solution.py:92
  106.2 2.4 copy-start.3
  123.4 4.1 collective-permute-start
  153.5 6.2 collective-permute-start.2
  185.6 70.6 %copy-start.5 = (bf16[64,1024]{1,0:T(8,128)(2,1)S(1)}, bf16[64,1024]{1,0:T(8,128)(2,1)}, u32[]{:S(2)}) copy-start(bf16[64,1024]{1,0:T(8,128)(2,1)} %param.17) | copy-start | bytes 393220
  185.6 13.7 %collective-permute-start.4 = (f32[1024]{0:T(1024)S(1)}, f32[1024]{0:T(1024)S(1)}, u32[]{:S(2)}, u32[]{:S(2)}) collective-permute-start(f32[1024]{0:T(1024)S(1)} %add.93), channel_id=1, source_target_pairs={{0,64},{16,80},{32,96},{48,112},{64,128},{80,144},{96,160},{112,17... | collective-permute-start | bytes 12296 | tf_op jit(solution)/shard_map/ppermute | solution.py:12
  223.5 3.9 collective-permute-start.5
  252.3 6.0 collective-permute-start.6
  282.6 10.5 %collective-permute-start.7 = (f32[1024]{0:T(1024)S(1)}, f32[1024]{0:T(1024)S(1)}, u32[]{:S(2)}, u32[]{:S(2)}) collective-permute-start(f32[1024]{0:T(1024)S(1)} %add.95), channel_id=1, source_target_pairs={{0,64},{16,80},{32,96},{48,112},{64,128},{80,144},{96,160},{112,17... | collective-permute-start | bytes 12296 | tf_op jit(solution)/shard_map/ppermute | solution.py:12
  317.4 6.7 collective-permute-start.8
  348.5 5.9 collective-permute-start.9
  378.7 6.9 collective-permute-start.10
  409.9 6.7 copy-start.4
  409.9 4.9 collective-permute-start.11
  424.8 4.1 copy-start.1
  436.1 4.4 collective-permute-start.12
  465.7 7.3 collective-permute-start.13
  497.9 6.2 collective-permute-start.14
  553.1 6.0 collective-permute-start.15
  656.1 8.9 %collective-permute-start.16 = (f32[1024]{0:T(1024)S(1)}, f32[1024]{0:T(1024)S(1)}, u32[]{:S(2)}, u32[]{:S(2)}) collective-permute-start(f32[1024]{0:T(1024)S(1)} %add.108), channel_id=1, source_target_pairs={{256,0},{272,16},{288,32},{304,48},{320,64},{336,80},{352,96},{368... | collective-permute-start | bytes 12296 | tf_op jit(solution)/shard_map/ppermute | solution.py:12
  858.2 9.9 %copy-start.2 = (bf16[1024,1024]{1,0:T(8,128)(2,1)S(1)}, bf16[1024,1024]{1,0:T(8,128)(2,1)}, u32[]{:S(2)}) copy-start(bf16[1024,1024]{1,0:T(8,128)(2,1)} %all-gather.8.cloned.1.call-done) | copy-start | bytes 6291460
  858.2 6.6 collective-permute-start.17
Sparse Core Ops, SparseCore 0:
  27.4 62.3 all-gather.3
  105.6 45.7 all-gather.5
  153.5 41.5 all-gather.7
where the time goes:
time: 899 us; the launch traced here: 881 us
  blocking collectives  599 us (67%)
  waiting for transfers between devices  100 us (11%)
  matrix products  89 us (10%)
  starting transfers between devices  58.2 us (6%)
  between operations  18.1 us (2%)
  local copies, waits for them, and re-layouts  10.5 us (1%)
    unnamed x25, blocking collectives  599 us
    all_gather x2, waiting for transfers between devices, local(): lax.all_gather(earlier_rows, 'state', axis=0, tiled=True)  62.5 us
    ppermute x18, starting transfers between devices, passed_along(): return lax.ppermute(block, axis, route)  57.9 us
    dot_general x47, matrix products, matvec(): jnp.dot(matrix, vector, precision=HIGH_PRECISION, preferred_element_type=...  48.1 us
    ppermute x18, waiting for transfers between devices, passed_along(): return lax.ppermute(block, axis, route)  37.4 us
  transfers between devices with their start and end apart: 21, of which 11 were waited for; matrix products, arithmetic and copies ran while one was open for 5% of the time, Pallas kernels for 0%

commit v1 on v0

v1 whole, which is shorter than its diff:
```python
import functools

import jax
import jax.numpy as jnp
from jax import lax
from jax.experimental import pallas as pl
from jax.experimental.pallas import tpu as pltpu
from jax.sharding import PartitionSpec as P

F32 = jnp.float32
BF16 = jnp.bfloat16
NT = (((1,), (1,)), ((), ()))


def pieces(x):
    hi = x.astype(BF16)
    rest = x - hi.astype(F32)
    mid = rest.astype(BF16)
    lo = (rest - mid.astype(F32)).astype(BF16)
    return hi, mid, lo


def times_transpose(rows, matrix):
    total = None
    for part in pieces(rows):
        term = lax.dot_general(part, matrix, NT, preferred_element_type=F32)
        total = term if total is None else total + term
    return total


def matvec_row(vector, matrix):
    hi, mid, lo = pieces(vector)
    width = vector.shape[1]
    row = lax.broadcasted_iota(jnp.int32, (8, width), 0)
    stacked = jnp.where(
        row == 0,
        hi.astype(F32),
        jnp.where(row == 1, mid.astype(F32), jnp.where(row == 2, lo.astype(F32), 0.0)),
    ).astype(BF16)
    out = lax.dot_general(stacked, matrix, NT, preferred_element_type=F32)
    return out[0:1] + out[1:2] + out[2:3]


def chain_kernel(w_ref, prior_ref, a_ref, g_ref, s_ref, y_ref, f_ref, sm_ref, p_ref):
    steps = y_ref.shape[0]

    def filter_step(k, state):
        predicted = matvec_row(state, a_ref[...])
        innovation = y_ref[pl.ds(k, 1), :] - predicted
        updated = predicted + w_ref[k] * matvec_row(innovation, g_ref[...])
        f_ref[pl.ds(k, 1), :] = updated
        return updated

    last = lax.fori_loop(0, steps, filter_step, prior_ref[...])
    p_ref[...] = times_transpose(f_ref[...], a_ref[...])
    sm_ref[pl.ds(steps - 1, 1), :] = last

    def smooth_step(j, later):
        k = steps - 2 - j
        value = f_ref[pl.ds(k, 1), :] + matvec_row(later - p_ref[pl.ds(k, 1), :], s_ref[...])
        sm_ref[pl.ds(k, 1), :] = value
        return value

    lax.fori_loop(0, steps - 1, smooth_step, last)


def run_chain(weights, prior, transition, gain, smoother, observed):
    steps, width = observed.shape
    vmem = pl.BlockSpec(memory_space=pltpu.VMEM)
    smem = pl.BlockSpec(memory_space=pltpu.SMEM)
    full = jax.ShapeDtypeStruct((steps, width), F32)
    return pl.pallas_call(
        chain_kernel,
        out_shape=(full, full),
        in_specs=[smem, vmem, vmem, vmem, vmem, vmem],
        out_specs=(vmem, vmem),
        scratch_shapes=[pltpu.VMEM((steps, width), F32)],
        compiler_params=pltpu.CompilerParams(vmem_limit_bytes=48 * 1024 * 1024),
    )(weights, prior, transition, gain, smoother, observed)


def local(prior, transition, gain, smoother, observed, present):
    panel = smoother.shape[0]
    seg = observed.shape[0]
    all_observed = lax.all_gather(observed, "tm", axis=0, tiled=True)
    weights = lax.all_gather(present.astype(F32), "tm", axis=0, tiled=True)
    smoother_full = lax.all_gather(smoother, "state", axis=0, tiled=True)
    filtered, smoothed = run_chain(
        weights, prior[None, :], transition, gain, smoother_full, all_observed
    )
    t0 = lax.axis_index("tm") * seg
    c0 = lax.axis_index("state") * panel
    block = lambda full: lax.dynamic_slice(full, (t0, c0), (seg, panel))
    return block(filtered), block(smoothed)


def solution(mesh):
    placed = (P(), P(), P(), P("state", None), P("tm", None), P("tm"))
    return jax.shard_map(
        local,
        mesh=mesh,
        in_specs=placed,
        out_specs=(P("tm", "state"), P("tm", "state")),
        check_vma=False,
    )
```

time: 899 us -> 400 us (0.44)
  the two profiles are of different devices: /device:TPU:1 before, /device:TPU:256 now
where the time goes in v1:
time: 400 us
  Pallas kernels  254 us (64%)
  blocking collectives  123 us (31%)
  between operations  14.7 us (4%)
  local copies, waits for them, and re-layouts  6.63 us (2%)
    pallas_call x1, Pallas kernels, run_chain(): pl.pallas_call(chain_kernel, out_shape=(full, full), in_specs=[smem, vmem...  254 us
    unnamed x1, blocking collectives  72.4 us
    all_gather x1, blocking collectives, local(): all_observed = lax.all_gather(observed, 'tm', axis=0, tiled=True)  50.5 us
  transfers between devices with their start and end apart: 1, of which 0 were waited for; matrix products, arithmetic and copies ran while one was open for 1% of the time, Pallas kernels for 0%

profile of v1, /device:TPU:256, one launch (start us, length us, event | category | flops | bytes accessed | tf_op | source)
XLA Modules:
  0.0 400.1 jit_solution(6018904509527883164)
XLA Ops:
  7.2 0.0 all-gather.3.cloned.1.call-start
  7.2 0.7 all-gather.3.cloned.1.call-update
  7.9 50.5 %all-gather = f32[32,4,1024]{2,1,0:T(4,128)S(1)} all-gather(f32[1,4,1024]{2,1,0:T(4,128)} %bitcast.4), channel_id=1, replica_groups=mesh['tm'=32,'state'=16] {'tm'}, dimensions={0}, use_global_device_ids=true | all-gather | bytes 540672 | tf_op jit(solution)/shard_map/all_gather | solution.py:85
  58.4 0.2 reshape.8.y_ref
  58.6 1.3 dynamic-slice
  60.5 0.8 convert_dynamic-update-slice_fusion
  61.3 72.4 %all-reduce.w_ref = f32[128]{0:T(128)S(1)} all-reduce(f32[128]{0:T(128)S(1)} %convert_dynamic-update-slice_fusion), channel_id=1, replica_groups=mesh['tm'=32,'state'=16] {'tm'}, use_global_device_ids=true, to_apply=%add | all-reduce | flops 128 | bytes 1024
  133.7 0.0 all-gather.3.cloned.1.call-done.s_ref
  133.7 0.0 copy-start
  133.7 1.6 copy-done
  135.3 0.0 copy-start.1
  135.3 1.6 copy-done.1
  136.9 0.0 copy-start.2
  136.9 0.7 copy-done.2
  137.6 254.4 %shard_map.77 = (f32[128,1024]{1,0:T(8,128)S(1)}, f32[128,1024]{1,0:T(8,128)S(1)}) custom-call(f32[128]{0:T(128)S(1)} %all-reduce.w_ref, f32[1,1024]{1,0:T(1,128)S(1)} %bitcast.3, bf16[1024,1024]{1,0:T(8,128)(2,1)S(1)} %copy-done, bf16[1024,1024]{1,0:T(8,128)(2,1)S(1)} %copy-done.1, bf16[1024,1024]{1,0:T(8,128)(2,1)} %all-gather.3.cloned.1.call-done.s_ref, ...), custom_call_target="tpu_custom_call" | custom-call | tf_op jit(solution)/shard_map/pallas_call | solution.py:72
  391.9 0.7 dynamic_slice.6
  392.6 0.7 dynamic_slice.7
  (1 shorter events, 0.0 us)
Async XLA Ops:
  7.2 126.5 %all-gather.3.cloned.1.call-start = ((), (), s32[]{:S(2)}) async-start(), calls=%async_computation | async-start | bytes 2228224 | tf_op jit(solution)/shard_map/all_gather | solution.py:87
  133.7 1.6 copy-start
  135.3 1.6 copy-start.1
  136.9 0.7 copy-start.2
Sparse Core Ops, SparseCore 0:
  10.1 41.7 all-gather.2

commit v2 on v1

--- a/solution.py
+++ b/solution.py
@@ -41,7 +41,7 @@
     return out[0:1] + out[1:2] + out[2:3]
 
 
-def chain_kernel(w_ref, prior_ref, a_ref, g_ref, s_ref, y_ref, f_ref, sm_ref, p_ref):
+def filter_kernel(w_ref, prior_ref, a_ref, g_ref, y_ref, f_ref):
     steps = y_ref.shape[0]
 
     def filter_step(k, state):
@@ -51,8 +51,13 @@
         f_ref[pl.ds(k, 1), :] = updated
         return updated
 
-    last = lax.fori_loop(0, steps, filter_step, prior_ref[...])
+    lax.fori_loop(0, steps, filter_step, prior_ref[...])
+
+
+def smooth_kernel(f_ref, a_ref, s_ref, sm_ref, p_ref):
+    steps = f_ref.shape[0]
     p_ref[...] = times_transpose(f_ref[...], a_ref[...])
+    last = f_ref[pl.ds(steps - 1, 1), :]
     sm_ref[pl.ds(steps - 1, 1), :] = last
 
     def smooth_step(j, later):
@@ -64,34 +69,100 @@
     lax.fori_loop(0, steps - 1, smooth_step, last)
 
 
-def run_chain(weights, prior, transition, gain, smoother, observed):
-    steps, width = observed.shape
+VMEM_LIMIT = 48 * 1024 * 1024
+
+
+def run_filter(weights, prior, transition, gain, observed):
     vmem = pl.BlockSpec(memory_space=pltpu.VMEM)
     smem = pl.BlockSpec(memory_space=pltpu.SMEM)
-    full = jax.ShapeDtypeStruct((steps, width), F32)
     return pl.pallas_call(
-        chain_kernel,
-        out_shape=(full, full),
-        in_specs=[smem, vmem, vmem, vmem, vmem, vmem],
-        out_specs=(vmem, vmem),
-        scratch_shapes=[pltpu.VMEM((steps, width), F32)],
-        compiler_params=pltpu.CompilerParams(vmem_limit_bytes=48 * 1024 * 1024),
-    )(weights, prior, transition, gain, smoother, observed)
+        filter_kernel,
+        out_shape=jax.ShapeDtypeStruct(observed.shape, F32),
+        in_specs=[smem, vmem, vmem, vmem, vmem],
+        out_specs=vmem,
+        compiler_params=pltpu.CompilerParams(vmem_limit_bytes=VMEM_LIMIT),
+    )(weights, prior, transition, gain, observed)
+
+
+def run_smoother(filtered, transition, smoother):
+    vmem = pl.BlockSpec(memory_space=pltpu.VMEM)
+    return pl.pallas_call(
+        smooth_kernel,
+        out_shape=jax.ShapeDtypeStruct(filtered.shape, F32),
+        in_specs=[vmem, vmem, vmem],
+        out_specs=vmem,
+        scratch_shapes=[pltpu.VMEM(filtered.shape, F32)],
+        compiler_params=pltpu.CompilerParams(vmem_limit_bytes=VMEM_LIMIT),
+    )(filtered, transition, smoother)
+
+
+def run_chain(weights, prior, transition, gain, smoother, observed):
+    filtered = run_filter(weights, prior, transition, gain, observed)
+    return filtered, run_smoother(filtered, transition, smoother)
+
+
+def gather_kernel(count, block_ref, out_ref, local_sem, send_sems, recv_sems):
+    me = lax.axis_index("tm")
+    mesh_id = pl.DeviceIdType.MESH
+    barrier = pltpu.get_barrier_semaphore()
+    for step in range(1, count):
+        peer = lax.rem(me + step, count)
+        pl.semaphore_signal(barrier, inc=1, device_id={"tm": peer}, device_id_type=mesh_id)
+    pl.semaphore_wait(barrier, count - 1)
+    own = pltpu.make_async_copy(block_ref, out_ref.at[me], local_sem)
+    own.start()
+    copies = []
+    for step in range(1, count):
+        peer = lax.rem(me + step, count)
+        copy = pltpu.make_async_remote_copy(
+            src_ref=block_ref,
+            dst_ref=out_ref.at[me],
+            send_sem=send_sems.at[step],
+            recv_sem=recv_sems.at[step],
+            device_id={"tm": peer},
+            device_id_type=mesh_id,
+        )
+        copy.start()
+        copies.append(copy)
+    for copy in copies:
+        copy.wait()
+    own.wait()
+
+
+def gather_over_time(block):
+    count = lax.axis_size("tm")
+    vmem = pl.BlockSpec(memory_space=pltpu.VMEM)
+    return pl.pallas_call(
+        functools.partial(gather_kernel, count),
+        out_shape=jax.ShapeDtypeStruct((count,) + block.shape, block.dtype),
+        in_specs=[vmem],
+        out_specs=vmem,
+        scratch_shapes=[
+            pltpu.SemaphoreType.DMA,
+            pltpu.SemaphoreType.DMA((count,)),
+            pltpu.SemaphoreType.DMA((count,)),
+        ],
+        compiler_params=pltpu.CompilerParams(collective_id=0, has_side_effects=True),
+    )(block)
 
 
 def local(prior, transition, gain, smoother, observed, present):
     panel = smoother.shape[0]
-    seg = observed.shape[0]
-    all_observed = lax.all_gather(observed, "tm", axis=0, tiled=True)
-    weights = lax.all_gather(present.astype(F32), "tm", axis=0, tiled=True)
+    seg, width = observed.shape
+    flags = jnp.broadcast_to(present.astype(F32)[:, None], (seg, 128))
+    block = jnp.concatenate([observed, flags], axis=1)
+    block = jnp.concatenate([block, jnp.zeros((8 - seg, width + 128), F32)], axis=0)
+    slots = gather_over_time(block)
+    all_observed = slots[:, :seg, :width].reshape(-1, width)
+    weights = slots[:, :seg, width].reshape(-1)
     smoother_full = lax.all_gather(smoother, "state", axis=0, tiled=True)
     filtered, smoothed = run_chain(
         weights, prior[None, :], transition, gain, smoother_full, all_observed
     )
     t0 = lax.axis_index("tm") * seg
     c0 = lax.axis_index("state") * panel
-    block = lambda full: lax.dynamic_slice(full, (t0, c0), (seg, panel))
-    return block(filtered), block(smoothed)
+    block_of = lambda full: lax.dynamic_slice(full, (t0, c0), (seg, panel))
+    return block_of(filtered), block_of(smoothed)
 
 
 def solution(mesh):

time: 400 us -> 316 us (0.79)
  the two profiles are of different devices: /device:TPU:256 before, /device:TPU:1 now
where the time goes in v2:
time: 316 us; the launch traced here: 315 us
  Pallas kernels  291 us (92%)
  between operations  14.1 us (4%)
  local copies, waits for them, and re-layouts  7.22 us (2%)
    pallas_call x1, Pallas kernels, run_filter(): pl.pallas_call(filter_kernel, out_shape=jax.ShapeDtypeStruct(observed.sha...  166 us
    pallas_call x1, Pallas kernels, run_smoother(): pl.pallas_call(smooth_kernel, out_shape=jax.ShapeDtypeStruct(filtered.sha...  86.9 us
    pallas_call x1, Pallas kernels, gather_over_time(): pl.pallas_call(functools.partial(gather_kernel, count), out_shape=jax.Sha...  37.6 us
  transfers between devices with their start and end apart: 1, of which 0 were waited for; matrix products, arithmetic and copies ran while one was open for 2% of the time, Pallas kernels for 65%

profile of v2, /device:TPU:1, one launch (start us, length us, event | category | flops | bytes accessed | tf_op | source)
XLA Modules:
  0.0 314.7 jit_solution(6301318054549191634)
XLA Ops:
  7.2 0.0 copy-start.3
  7.2 0.0 copy-start
  7.2 0.0 all-gather.2.cloned.1.call-start
  7.2 0.7 all-gather.2.cloned.1.call-update
  7.9 0.7 convert_element_type.3
  8.6 0.1 broadcast_in_dim.4
  8.7 1.3 select_maximum_fusion.block_ref
  10.0 37.6 %shard_map.77 = f32[32,8,1152]{2,1,0:T(8,128)} custom-call(f32[8,1152]{1,0:T(8,128)} %select_maximum_fusion.block_ref), custom_call_target="tpu_custom_call" | custom-call | tf_op jit(solution)/shard_map/pallas_call | solution.py:135
  47.6 1.3 slice.7
  49.0 0.2 reshape.8.y_ref
  49.1 1.0 slice_reduce_fusion
  50.2 0.1 reshape_squeeze.3.w_ref
  50.3 0.0 copy-done.3
  50.3 0.0 copy-done
  50.3 0.0 copy-start.1
  50.3 1.6 copy-done.1
  51.9 166.1 %shard_map.78.f_ref = f32[128,1024]{1,0:T(8,128)S(1)} custom-call(f32[128]{0:T(128)S(1)} %reshape_squeeze.3.w_ref, f32[1,1024]{1,0:T(1,128)S(1)} %bitcast.1, bf16[1024,1024]{1,0:T(8,128)(2,1)S(1)} %copy-done, bf16[1024,1024]{1,0:T(8,128)(2,1)S(1)} %copy-done.1, f32[128,1024]{1,0:T(8,128)S(1)} %reshape.8.y_ref), custom_call_target="tpu_custom_call" | custom-call | tf_op jit(solution)/shard_map/pallas_call | solution.py:78
  218.1 0.7 dynamic_slice.6
  218.7 0.0 all-gather.2.cloned.1.call-done.s_ref
  218.7 0.0 copy-start.2
  218.7 1.6 copy-done.2
  220.3 86.9 %shard_map.79 = f32[128,1024]{1,0:T(8,128)S(1)} custom-call(f32[128,1024]{1,0:T(8,128)S(1)} %shard_map.78.f_ref, bf16[1024,1024]{1,0:T(8,128)(2,1)S(1)} %copy-done, bf16[1024,1024]{1,0:T(8,128)(2,1)S(1)} %copy-done.2), custom_call_target="tpu_custom_call" | custom-call | tf_op jit(solution)/shard_map/pallas_call | solution.py:89
  307.2 0.7 dynamic_slice.7
Async XLA Ops:
  7.2 43.1 %copy-start.3 = (f32[1024]{0:T(1024)S(1)}, f32[1024]{0:T(1024)}, u32[]{:S(2)}) copy-start(f32[1024]{0:T(1024)} %param.6) | copy-start | bytes 12292
  7.2 43.1 %copy-start = (bf16[1024,1024]{1,0:T(8,128)(2,1)S(1)}, bf16[1024,1024]{1,0:T(8,128)(2,1)}, u32[]{:S(2)}) copy-start(bf16[1024,1024]{1,0:T(8,128)(2,1)} %a_ref.3) | copy-start | bytes 6291460
  7.2 211.5 %all-gather.2.cloned.1.call-start = ((), (), s32[]{:S(2)}) async-start(), calls=%async_computation | async-start | bytes 2228224 | tf_op jit(solution)/shard_map/all_gather | solution.py:158
  50.3 1.6 copy-start.1
  218.7 1.6 copy-start.2
Sparse Core Ops, SparseCore 0:
  10.1 48.9 all-gather.1

commit v3 on v2

--- a/solution.py
+++ b/solution.py
@@ -41,64 +41,104 @@
     return out[0:1] + out[1:2] + out[2:3]
 
 
-def filter_kernel(w_ref, prior_ref, a_ref, g_ref, y_ref, f_ref):
-    steps = y_ref.shape[0]
-
-    def filter_step(k, state):
-        predicted = matvec_row(state, a_ref[...])
-        innovation = y_ref[pl.ds(k, 1), :] - predicted
-        updated = predicted + w_ref[k] * matvec_row(innovation, g_ref[...])
-        f_ref[pl.ds(k, 1), :] = updated
+def column_from_row(matrix, row):
+    return jnp.sum(matrix * row, axis=1, keepdims=True)
+
+
+def row_from_column(matrix_t, column):
+    return jnp.sum(matrix_t * column, axis=0, keepdims=True)
+
+
+def filter_kernel(
+    flag_ref, prior_ref, w_ref, y_ref, a_ref, g_ref, pair_ref, pair_t_ref,
+    even_ref, odd_ref, extra_ref, prev_ref,
+):
+    half = y_ref.shape[1]
+    gain = g_ref[...]
+    transition = a_ref[...]
+    w_even, w_odd = w_ref[0], w_ref[1]
+    y_even, y_odd = y_ref[0], y_ref[1]
+    corr_even = w_even * times_transpose(y_even, gain)
+    corr_odd = w_odd * times_transpose(y_odd, gain)
+    moved = times_transpose(corr_even, transition)
+    extra_ref[...] = moved - w_odd * times_transpose(moved, gain) + corr_odd
+
+    def pair_step(i, state):
+        middle = column_from_row(pair_ref[flag_ref[2 * i]], state)
+        updated = row_from_column(pair_t_ref[flag_ref[2 * i + 1]], middle)
+        updated = updated + extra_ref[pl.ds(i, 1), :]
+        odd_ref[pl.ds(i, 1), :] = updated
         return updated
 
-    lax.fori_loop(0, steps, filter_step, prior_ref[...])
-
-
-def smooth_kernel(f_ref, a_ref, s_ref, sm_ref, p_ref):
-    steps = f_ref.shape[0]
-    p_ref[...] = times_transpose(f_ref[...], a_ref[...])
-    last = f_ref[pl.ds(steps - 1, 1), :]
-    sm_ref[pl.ds(steps - 1, 1), :] = last
-
-    def smooth_step(j, later):
-        k = steps - 2 - j
-        value = f_ref[pl.ds(k, 1), :] + matvec_row(later - p_ref[pl.ds(k, 1), :], s_ref[...])
-        sm_ref[pl.ds(k, 1), :] = value
+    lax.fori_loop(0, half, pair_step, prior_ref[...])
+    prev_ref[0:1, :] = prior_ref[...]
+    prev_ref[1:half, :] = odd_ref[0 : half - 1, :]
+    predicted = times_transpose(prev_ref[...], transition)
+    even_ref[...] = predicted + w_even * times_transpose(y_even - predicted, gain)
+
+
+def smooth_kernel(
+    even_ref, odd_ref, a_ref, s_ref, s32_ref, s32_t_ref,
+    s_even_ref, s_odd_ref, extra_ref, d_even_ref,
+):
+    half = even_ref.shape[0]
+    smoother = s_ref[...]
+    transition = a_ref[...]
+    f_even, f_odd = even_ref[...], odd_ref[...]
+    d_even_ref[...] = f_even - times_transpose(times_transpose(f_even, transition), smoother)
+    d_odd = f_odd - times_transpose(times_transpose(f_odd, transition), smoother)
+    pulled = times_transpose(d_even_ref[...], smoother)
+    extra_ref[0 : half - 1, :] = pulled[1:half, :] + d_odd[0 : half - 1, :]
+    last = odd_ref[half - 1 : half, :]
+    s_odd_ref[half - 1 : half, :] = last
+
+    def pair_step(j, state):
+        r = half - 2 - j
+        middle = column_from_row(s32_ref[...], state)
+        value = row_from_column(s32_t_ref[...], middle) + extra_ref[pl.ds(r, 1), :]
+        s_odd_ref[pl.ds(r, 1), :] = value
         return value
 
-    lax.fori_loop(0, steps - 1, smooth_step, last)
-
-
-VMEM_LIMIT = 48 * 1024 * 1024
-
-
-def run_filter(weights, prior, transition, gain, observed):
+    lax.fori_loop(0, half - 1, pair_step, last)
+    s_even_ref[...] = times_transpose(s_odd_ref[...], smoother) + d_even_ref[...]
+
+
+VMEM_LIMIT = 60 * 1024 * 1024
+
+
+def run_chain(weights, prior, transition, gain, smoother, observed):
+    steps, width = observed.shape
+    half = steps // 2
     vmem = pl.BlockSpec(memory_space=pltpu.VMEM)
     smem = pl.BlockSpec(memory_space=pltpu.SMEM)
-    return pl.pallas_call(
+    params = pltpu.CompilerParams(vmem_limit_bytes=VMEM_LIMIT)
+    flags = weights.astype(jnp.int32)
+    w_pair = weights.reshape(half, 2).T[:, :, None]
+    y_pair = observed.reshape(half, 2, width).transpose(1, 0, 2)
+    a32 = transition.astype(F32)
+    b32 = a32 - jnp.dot(gain, transition, preferred_element_type=F32)
+    pair = jnp.stack([a32, b32])
+    pair_t = jnp.stack([a32.T, b32.T])
+    rows = jax.ShapeDtypeStruct((half, width), F32)
+    f_even, f_odd = pl.pallas_call(
         filter_kernel,
-        out_shape=jax.ShapeDtypeStruct(observed.shape, F32),
-        in_specs=[smem, vmem, vmem, vmem, vmem],
-        out_specs=vmem,
-        compiler_params=pltpu.CompilerParams(vmem_limit_bytes=VMEM_LIMIT),
-    )(weights, prior, transition, gain, observed)
-
-
-def run_smoother(filtered, transition, smoother):
-    vmem = pl.BlockSpec(memory_space=pltpu.VMEM)
-    return pl.pallas_call(
+        out_shape=(rows, rows),
+        in_specs=[smem] + [vmem] * 7,
+        out_specs=(vmem, vmem),
+        scratch_shapes=[pltpu.VMEM((half, width), F32)] * 2,
+        compiler_params=params,
+    )(flags, prior, w_pair, y_pair, transition, gain, pair, pair_t)
+    s32 = smoother.astype(F32)
+    s_even, s_odd = pl.pallas_call(
         smooth_kernel,
-        out_shape=jax.ShapeDtypeStruct(filtered.shape, F32),
-        in_specs=[vmem, vmem, vmem],
-        out_specs=vmem,
-        scratch_shapes=[pltpu.VMEM(filtered.shape, F32)],
-        compiler_params=pltpu.CompilerParams(vmem_limit_bytes=VMEM_LIMIT),
-    )(filtered, transition, smoother)
-
-
-def run_chain(weights, prior, transition, gain, smoother, observed):
-    filtered = run_filter(weights, prior, transition, gain, observed)
-    return filtered, run_smoother(filtered, transition, smoother)
+        out_shape=(rows, rows),
+        in_specs=[vmem] * 6,
+        out_specs=(vmem, vmem),
+        scratch_shapes=[pltpu.VMEM((half, width), F32)] * 2,
+        compiler_params=params,
+    )(f_even, f_odd, transition, smoother, s32, s32.T)
+    interleave = lambda even, odd: jnp.stack([even, odd], axis=1).reshape(steps, width)
+    return interleave(f_even, f_odd), interleave(s_even, s_odd)
 
 
 def gather_kernel(count, block_ref, out_ref, local_sem, send_sems, recv_sems):

time: 316 us -> 212 us (0.67)
  Pallas kernels: 291 us -> 143 us
  other arithmetic: 1.99 us -> 21.9 us
  local copies, waits for them, and re-layouts: 7.22 us -> 26.9 us
  matrix products: 0 us -> 4.42 us
    pallas_call x2, Pallas kernels: 253 us -> 105 us  [the longest x1 54.4 us: run_chain(): pl.pallas_call(filter_kernel, out_shape=(rows, rows), in_specs=[smem] + [...]
    another operation x0 -> x5, other arithmetic: none -> 17.3 us  [the longest x2 11.1 us: run_chain(): pair_t = jnp.stack([a32.T, b32.T])]
    another operation x1 -> x6, local copies, waits for them, and re-layouts: 0.1 us -> 11.1 us  [the longest x1 8.81 us: run_chain(): pair = jnp.stack([a32, b32])]
    dot_general x0 -> x1, matrix products: none -> 4.42 us  [run_chain(): b32 = a32 - jnp.dot(gain, transition, preferred_element_type=F32)]
    convert_element_type x0 -> x2, local copies, waits for them, and re-layouts: none -> 3.62 us  [the longest x1 3 us: run_chain(): s32 = smoother.astype(F32)]
  transfers between devices with their start and end apart: 1 -> 1, of which waited for: 0 -> 0; matrix products, arithmetic and copies ran while one was open for 2% -> 20% of each run, Pallas kernels for 65% -> 44%
where the time goes in v3:
time: 212 us; the launch traced here: 211 us
  Pallas kernels  143 us (67%)
  local copies, waits for them, and re-layouts  26.9 us (13%)
  other arithmetic  21.9 us (10%)
  between operations  14.2 us (7%)
  matrix products  4.42 us (2%)
    pallas_call x1, Pallas kernels, run_chain(): pl.pallas_call(filter_kernel, out_shape=(rows, rows), in_specs=[smem] + [...  54.4 us
    pallas_call x1, Pallas kernels, run_chain(): pl.pallas_call(smooth_kernel, out_shape=(rows, rows), in_specs=[vmem] * 6...  51.1 us
    pallas_call x1, Pallas kernels, gather_over_time(): pl.pallas_call(functools.partial(gather_kernel, count), out_shape=jax.Sha...  37.6 us
    another operation x2, other arithmetic, run_chain(): pair_t = jnp.stack([a32.T, b32.T])  11.1 us
    another operation x1, local copies, waits for them, and re-layouts, run_chain(): pair = jnp.stack([a32, b32])  8.81 us
    dot_general x1, matrix products, run_chain(): b32 = a32 - jnp.dot(gain, transition, preferred_element_type=F32)  4.42 us
  transfers between devices with their start and end apart: 1, of which 0 were waited for; matrix products, arithmetic and copies ran while one was open for 20% of the time, Pallas kernels for 44%

profile of v3, /device:TPU:1, one launch (start us, length us, event | category | flops | bytes accessed | tf_op | source)
XLA Modules:
  0.0 211.2 jit_solution(4520588698371434074)
XLA Ops:
  7.2 0.7 all-gather.2.cloned.1.call-update
  7.9 2.9 %copy.29 = bf16[1024,1024]{0,1:T(8,128)(2,1)S(1)} copy(bf16[1024,1024]{1,0:T(8,128)(2,1)} %a_ref.3) | data formatting | bytes 4194304 | tf_op args[1]
  10.8 2.8 %convert_bitcast_fusion = (f32[1,1024,1024]{2,1,0:T(8,128)}, f32[1,1024,1024]{1,2,0:T(8,128)S(1)}) fusion(bf16[1024,1024]{0,1:T(8,128)(2,1)S(1)} %copy.29), kind=kLoop, calls=%fused_computation.2 | loop fusion | flops 1048576 | bytes 10485760 | tf_op jit(solution)/shard_map/stack | solution.py:121
  13.6 0.9 copy-done.1
  14.5 4.4 %fusion = (f32[1,1024,1024]{2,1,0:T(8,128)}, f32[1,1024,1024]{1,2,0:T(8,128)S(1)}) fusion(bf16[1024,1024]{0,1:T(8,128)(2,1)S(1)} %copy.29, bf16[1024,1024]{1,0:T(8,128)(2,1)S(1)} %copy-done.1, bf16[1024,1024]{1,0:T(8,128)(2,1)S(1)} %copy-done), kind=kOutput, calls=%fused_computation.5 | convolution fusion | flops 2149580800 | bytes 14680064 | tf_op jit(solution)/shard_map/dot_general | solution.py:119
  18.9 4.1 %pad_maximum_fusion = f32[2,1024,1024]{1,2,0:T(8,128)} fusion(f32[1,1024,1024]{1,2,0:T(8,128)S(1)} %get-tuple-element.11, f32[1,1024,1024]{1,2,0:T(8,128)S(1)} %get-tuple-element.13), kind=kLoop, calls=%fused_computation | loop fusion | flops 2097152 | bytes 16777216 | tf_op jit(solution)/shard_map/stack | solution.py:120
  23.0 8.8 %copy.32.pair_ref = f32[2,1024,1024]{2,1,0:T(8,128)} copy(f32[2,1024,1024]{1,2,0:T(8,128)} %pad_maximum_fusion) | data formatting | bytes 16777216 | tf_op jit(solution)/shard_map/stack | solution.py:120
  31.8 0.1 broadcast_in_dim.6
  31.9 0.6 select_maximum_fusion.block_ref
  32.5 37.6 %shard_map.77 = f32[32,8,1152]{2,1,0:T(8,128)} custom-call(f32[8,1152]{1,0:T(8,128)} %select_maximum_fusion.block_ref), custom_call_target="tpu_custom_call" | custom-call | tf_op jit(solution)/shard_map/pallas_call | solution.py:175
  70.1 1.3 slice.7
  71.4 0.4 reshape_reshape.3
  71.8 1.0 copy.41
  72.8 1.0 slice_reduce_fusion
  73.8 0.1 reshape_reshape_squeeze.3
  73.9 1.1 copy.31.w_ref
  75.0 1.5 convert_reduce_fusion
  76.6 0.6 convert_element_type.16.flag_ref
  77.2 8.3 %pad_maximum_fusion.1.pair_t_ref = f32[2,1024,1024]{2,1,0:T(8,128)} fusion(f32[1,1024,1024]{2,1,0:T(8,128)} %get-tuple-element.10, f32[1,1024,1024]{2,1,0:T(8,128)} %get-tuple-element.12), kind=kLoop, calls=%fused_computation.1 | loop fusion | flops 2097152 | bytes 16777216 | tf_op jit(solution)/shard_map/stack | solution.py:121
  85.5 54.4 %shard_map.78 = (f32[64,1024]{1,0:T(8,128)}, f32[64,1024]{1,0:T(8,128)}) custom-call(s32[128]{0:T(128)} %convert_element_type.16.flag_ref, f32[1,1024]{1,0:T(1,128)} %bitcast.33, f32[2,64,1]{2,1,0:T(8,128)} %copy.31.w_ref, f32[2,64,1024]{2,1,0:T(8,128)} %bitcast.27, bf16[1024,1024]{1,0:T(8,128)(2,1)} %a_ref.3, bf16[1024,1024]{1,0:T(8,128)(2,1)} %g_ref.1, ...), custom_call_target="tpu_custom_call" | custom-call | tf_op jit(solution)/shard_map/pallas_call | solution.py:123
  139.9 1.1 pad_maximum_fusion.2
  141.0 0.4 copy.33
  141.4 0.4 reshape.12
  141.8 0.7 dynamic_slice.6
  142.4 2.9 %copy.34 = bf16[1024,1024]{0,1:T(8,128)(2,1)S(1)} copy(bf16[1024,1024]{1,0:T(8,128)(2,1)} %all-gather.2.cloned.1.call-done.s_ref) | data formatting | bytes 4194304 | tf_op jit(solution)/shard_map/all_gather | solution.py:198
  145.3 2.4 %convert_bitcast_fusion.2.s32_t_ref = f32[1024,1024]{1,0:T(8,128)} fusion(bf16[1024,1024]{0,1:T(8,128)(2,1)S(1)} %copy.34), kind=kLoop, calls=%fused_computation.7 | loop fusion | flops 1048576 | bytes 6291456 | tf_op jit(solution)/shard_map/transpose | solution.py:139
  147.7 3.0 %copy.35.s32_ref = f32[1024,1024]{1,0:T(8,128)} copy(bf16[1024,1024]{0,1:T(8,128)(2,1)S(1)} %copy.34) | data formatting | bytes 6291456 | tf_op jit(solution)/shard_map/convert_element_type | solution.py:131
  150.7 51.1 %shard_map.79 = (f32[64,1024]{1,0:T(8,128)}, f32[64,1024]{1,0:T(8,128)}) custom-call(f32[64,1024]{1,0:T(8,128)} %get-tuple-element.6.even_ref, f32[64,1024]{1,0:T(8,128)} %get-tuple-element.7.odd_ref, bf16[1024,1024]{1,0:T(8,128)(2,1)} %a_ref.3, bf16[1024,1024]{1,0:T(8,128)(2,1)} %all-gather.2.cloned.1.call-done.s_ref, f32[1024,1024]{1,0:T(8,128)} %copy.35.s32_ref, ...), custom_call_target="tpu_custom_call" | custom-call | tf_op jit(solution)/shard_map/pallas_call | solution.py:132
  201.8 1.1 pad_maximum_fusion.3
  202.9 0.4 copy.36
  203.3 0.4 reshape.13
  203.7 0.7 dynamic_slice.7
  (10 shorter events, 0.1 us)
Async XLA Ops:
  7.2 135.3 %all-gather.2.cloned.1.call-start = ((), (), s32[]{:S(2)}) async-start(), calls=%async_computation | async-start | bytes 2228224 | tf_op jit(solution)/shard_map/all_gather | solution.py:198
  10.8 2.8 %copy-start = (bf16[1024,1024]{1,0:T(8,128)(2,1)S(1)}, bf16[1024,1024]{1,0:T(8,128)(2,1)}, u32[]{:S(2)}) copy-start(bf16[1024,1024]{1,0:T(8,128)(2,1)} %a_ref.3) | copy-start | bytes 6291460
  10.8 3.7 %copy-start.1 = (bf16[1024,1024]{1,0:T(8,128)(2,1)S(1)}, bf16[1024,1024]{1,0:T(8,128)(2,1)}, u32[]{:S(2)}) copy-start(bf16[1024,1024]{1,0:T(8,128)(2,1)} %g_ref.1) | copy-start | bytes 6291460
  23.0 8.8 %copy-start.3 = (s32[4]{0:T(128)S(1)}, s32[4]{0:T(128)}, u32[]{:S(2)}) copy-start(s32[4]{0:T(128)} %param.11) | copy-start | bytes 52
  23.0 8.9 %copy-start.2 = (f32[4,1024]{1,0:T(4,128)S(1)}, f32[4,1024]{1,0:T(4,128)}, u32[]{:S(2)}) copy-start(f32[4,1024]{1,0:T(4,128)} %param.10) | copy-start | bytes 49156
Sparse Core Ops, SparseCore 0:
  10.1 49.0 all-gather.1

commit v4 on v3

--- a/solution.py
+++ b/solution.py
@@ -49,11 +49,31 @@
     return jnp.sum(matrix_t * column, axis=0, keepdims=True)
 
 
+BAND = 256
+
+
+def build_pairs(a_ref, g_ref, a_t_ref, g_t_ref, pair_ref, pair_t_ref):
+    width = a_ref.shape[0]
+    for start in range(0, width, BAND):
+        rows = slice(start, start + BAND)
+        a_rows = a_ref[rows, :].astype(F32)
+        pair_ref[0, rows, :] = a_rows
+        pair_ref[1, rows, :] = a_rows - jnp.dot(
+            g_ref[rows, :], a_ref[...], preferred_element_type=F32
+        )
+        a_t_rows = a_t_ref[rows, :].astype(F32)
+        pair_t_ref[0, rows, :] = a_t_rows
+        pair_t_ref[1, rows, :] = a_t_rows - jnp.dot(
+            a_t_ref[rows, :], g_t_ref[...], preferred_element_type=F32
+        )
+
+
 def filter_kernel(
-    flag_ref, prior_ref, w_ref, y_ref, a_ref, g_ref, pair_ref, pair_t_ref,
-    even_ref, odd_ref, extra_ref, prev_ref,
+    flag_ref, prior_ref, w_ref, y_ref, a_ref, g_ref, a_t_ref, g_t_ref,
+    even_ref, odd_ref, extra_ref, prev_ref, pair_ref, pair_t_ref,
 ):
     half = y_ref.shape[1]
+    build_pairs(a_ref, g_ref, a_t_ref, g_t_ref, pair_ref, pair_t_ref)
     gain = g_ref[...]
     transition = a_ref[...]
     w_even, w_odd = w_ref[0], w_ref[1]
@@ -78,10 +98,15 @@
 
 
 def smooth_kernel(
-    even_ref, odd_ref, a_ref, s_ref, s32_ref, s32_t_ref,
-    s_even_ref, s_odd_ref, extra_ref, d_even_ref,
+    even_ref, odd_ref, a_ref, s_ref, s_t_ref,
+    s_even_ref, s_odd_ref, extra_ref, d_even_ref, s32_ref, s32_t_ref,
 ):
     half = even_ref.shape[0]
+    width = s_ref.shape[0]
+    for start in range(0, width, BAND):
+        rows = slice(start, start + BAND)
+        s32_ref[rows, :] = s_ref[rows, :].astype(F32)
+        s32_t_ref[rows, :] = s_t_ref[rows, :].astype(F32)
     smoother = s_ref[...]
     transition = a_ref[...]
     f_even, f_odd = even_ref[...], odd_ref[...]
@@ -115,28 +140,25 @@
     flags = weights.astype(jnp.int32)
     w_pair = weights.reshape(half, 2).T[:, :, None]
     y_pair = observed.reshape(half, 2, width).transpose(1, 0, 2)
-    a32 = transition.astype(F32)
-    b32 = a32 - jnp.dot(gain, transition, preferred_element_type=F32)
-    pair = jnp.stack([a32, b32])
-    pair_t = jnp.stack([a32.T, b32.T])
     rows = jax.ShapeDtypeStruct((half, width), F32)
+    square = pltpu.VMEM((width, width), F32)
+    stacked = pltpu.VMEM((2, width, width), F32)
     f_even, f_odd = pl.pallas_call(
         filter_kernel,
         out_shape=(rows, rows),
         in_specs=[smem] + [vmem] * 7,
         out_specs=(vmem, vmem),
-        scratch_shapes=[pltpu.VMEM((half, width), F32)] * 2,
+        scratch_shapes=[pltpu.VMEM((half, width), F32)] * 2 + [stacked, stacked],
         compiler_params=params,
-    )(flags, prior, w_pair, y_pair, transition, gain, pair, pair_t)
-    s32 = smoother.astype(F32)
+    )(flags, prior, w_pair, y_pair, transition, gain, transition.T, gain.T)
     s_even, s_odd = pl.pallas_call(
         smooth_kernel,
         out_shape=(rows, rows),
-        in_specs=[vmem] * 6,
+        in_specs=[vmem] * 5,
         out_specs=(vmem, vmem),
-        scratch_shapes=[pltpu.VMEM((half, width), F32)] * 2,
+        scratch_shapes=[pltpu.VMEM((half, width), F32)] * 2 + [square, square],
         compiler_params=params,
-    )(f_even, f_odd, transition, smoother, s32, s32.T)
+    )(f_even, f_odd, transition, smoother, smoother.T)
     interleave = lambda even, odd: jnp.stack([even, odd], axis=1).reshape(steps, width)
     return interleave(f_even, f_odd), interleave(s_even, s_odd)
 

time: 212 us -> 183 us (0.86)
  other arithmetic: 21.9 us -> 5.67 us
  local copies, waits for them, and re-layouts: 26.9 us -> 19 us
  matrix products: 4.42 us -> 0 us
    another operation x3 -> x0, other arithmetic: 15.2 us -> none  [the longest x2 11.1 us: run_chain(): pair_t = jnp.stack([a32.T, b32.T])]
    another operation x1 -> x0, local copies, waits for them, and re-layouts: 8.81 us -> none  [run_chain(): pair = jnp.stack([a32, b32])]
    dot_general x1 -> x0, matrix products: 4.42 us -> none  [run_chain(): b32 = a32 - jnp.dot(gain, transition, preferred_element_type=F32)]
    convert_element_type x1 -> x0, local copies, waits for them, and re-layouts: 3 us -> none  [run_chain(): s32 = smoother.astype(F32)]
    unnamed x9 -> x4, local copies, waits for them, and re-layouts: 3.8 us -> 6.55 us
    transpose x1 -> x0, other arithmetic: 2.44 us -> none  [run_chain(): s_even, s_odd = pl.pallas_call(smooth_kernel, out_shape=(rows, rows), in_...]
  transfers between devices with their start and end apart: 1 -> 1, of which waited for: 0 -> 0; matrix products, arithmetic and copies ran while one was open for 20% -> 10% of each run, Pallas kernels for 44% -> 51%
where the time goes in v4:
time: 183 us; the launch traced here: 182 us
  Pallas kernels  143 us (78%)
  local copies, waits for them, and re-layouts  19 us (10%)
  between operations  14.1 us (8%)
  other arithmetic  5.67 us (3%)
    pallas_call x1, Pallas kernels, run_chain(): pl.pallas_call(filter_kernel, out_shape=(rows, rows), in_specs=[smem] + [...  55.2 us
    pallas_call x1, Pallas kernels, run_chain(): pl.pallas_call(smooth_kernel, out_shape=(rows, rows), in_specs=[vmem] * 5...  49.8 us
    pallas_call x1, Pallas kernels, gather_over_time(): pl.pallas_call(functools.partial(gather_kernel, count), out_shape=jax.Sha...  37.8 us
    unnamed x4, local copies, waits for them, and re-layouts  6.55 us
    all_gather x1, local copies, waits for them, and re-layouts, local(): smoother_full = lax.all_gather(smoother, 'state', axis=0, tiled=True)  3.95 us
  transfers between devices with their start and end apart: 1, of which 0 were waited for; matrix products, arithmetic and copies ran while one was open for 10% of the time, Pallas kernels for 51%

profile of v4, /device:TPU:1, one launch (start us, length us, event | category | flops | bytes accessed | tf_op | source)
XLA Modules:
  0.0 182.2 jit_solution(1612628626687595679)
XLA Ops:
  7.2 0.0 all-gather.2.cloned.1.call-start
  7.2 0.7 all-gather.2.cloned.1.call-update
  7.9 0.7 convert_element_type.8
  8.6 0.1 broadcast_in_dim.6
  8.6 1.3 select_maximum_fusion.block_ref
  10.0 0.0 copy-start
  10.0 37.8 %shard_map.77 = f32[32,8,1152]{2,1,0:T(8,128)} custom-call(f32[8,1152]{1,0:T(8,128)} %select_maximum_fusion.block_ref), custom_call_target="tpu_custom_call" | custom-call | tf_op jit(solution)/shard_map/pallas_call | solution.py:197
  47.8 1.3 slice.7
  49.1 0.4 reshape_reshape.3
  49.5 1.0 copy.34
  50.5 1.0 slice_reduce_fusion
  51.5 0.1 reshape_reshape_squeeze.3
  51.6 1.1 copy.27.w_ref
  52.7 1.5 convert_reduce_fusion
  54.2 0.6 convert_element_type.10.flag_ref
  54.8 0.0 copy-done
  54.8 2.6 %copy.25 = bf16[1024,1024]{0,1:T(8,128)(2,1)} copy(bf16[1024,1024]{1,0:T(8,128)(2,1)S(1)} %copy-done) | data formatting | bytes 4194304 | tf_op args[1]
  57.5 3.9 %copy.26 = bf16[1024,1024]{0,1:T(8,128)(2,1)} copy(bf16[1024,1024]{1,0:T(8,128)(2,1)} %g_ref.1) | data formatting | bytes 4194304 | tf_op args[2]
  61.4 55.2 %shard_map.78 = (f32[64,1024]{1,0:T(8,128)}, f32[64,1024]{1,0:T(8,128)}) custom-call(s32[128]{0:T(128)} %convert_element_type.10.flag_ref, f32[1,1024]{1,0:T(1,128)} %bitcast.23, f32[2,64,1]{2,1,0:T(8,128)} %copy.27.w_ref, f32[2,64,1024]{2,1,0:T(8,128)} %bitcast.17, bf16[1024,1024]{1,0:T(8,128)(2,1)} %a_ref.3, bf16[1024,1024]{1,0:T(8,128)(2,1)} %g_ref.1, ...), custom_call_target="tpu_custom_call" | custom-call | tf_op jit(solution)/shard_map/pallas_call | solution.py:146
  116.6 1.1 pad_maximum_fusion
  117.7 0.4 copy.28
  118.1 0.4 reshape.12
  118.4 0.7 dynamic_slice.6
  119.1 0.0 all-gather.2.cloned.1.call-done.s_ref
  119.1 3.9 %copy.29 = bf16[1024,1024]{0,1:T(8,128)(2,1)} copy(bf16[1024,1024]{1,0:T(8,128)(2,1)} %all-gather.2.cloned.1.call-done.s_ref) | data formatting | bytes 4194304 | tf_op jit(solution)/shard_map/all_gather | solution.py:220
  123.1 49.8 %shard_map.79 = (f32[64,1024]{1,0:T(8,128)}, f32[64,1024]{1,0:T(8,128)}) custom-call(f32[64,1024]{1,0:T(8,128)} %get-tuple-element.6.even_ref, f32[64,1024]{1,0:T(8,128)} %get-tuple-element.7.odd_ref, bf16[1024,1024]{1,0:T(8,128)(2,1)} %a_ref.3, bf16[1024,1024]{1,0:T(8,128)(2,1)} %all-gather.2.cloned.1.call-done.s_ref, bf16[1024,1024]{1,0:T(8,128)(2,1)} %bitcast.14), custom_call_target="tpu_custom_call" | custom-call | tf_op jit(solution)/shard_map/pallas_call | solution.py:154
  172.9 1.1 pad_maximum_fusion.1
  174.0 0.4 copy.30
  174.4 0.4 reshape.13
  174.7 0.7 dynamic_slice.7
Async XLA Ops:
  7.2 111.9 %all-gather.2.cloned.1.call-start = ((), (), s32[]{:S(2)}) async-start(), calls=%async_computation | async-start | bytes 2228224 | tf_op jit(solution)/shard_map/all_gather | solution.py:220
  10.0 44.9 %copy-start = (bf16[1024,1024]{1,0:T(8,128)(2,1)S(1)}, bf16[1024,1024]{1,0:T(8,128)(2,1)}, u32[]{:S(2)}) copy-start(bf16[1024,1024]{1,0:T(8,128)(2,1)} %a_ref.3) | copy-start | bytes 6291460
Sparse Core Ops, SparseCore 0:
  10.1 48.9 all-gather.1

commit v5 on v4

--- a/solution.py
+++ b/solution.py
@@ -52,7 +52,14 @@
 BAND = 256
 
 
-def build_pairs(a_ref, g_ref, a_t_ref, g_t_ref, pair_ref, pair_t_ref):
+def transpose_into(dst, src):
+    width = src.shape[0]
+    for i in range(0, width, BAND):
+        for j in range(0, width, BAND):
+            dst[j : j + BAND, i : i + BAND] = src[i : i + BAND, j : j + BAND].T
+
+
+def build_pairs(a_ref, g_ref, pair_ref, pair_t_ref):
     width = a_ref.shape[0]
     for start in range(0, width, BAND):
         rows = slice(start, start + BAND)
@@ -61,19 +68,16 @@
         pair_ref[1, rows, :] = a_rows - jnp.dot(
             g_ref[rows, :], a_ref[...], preferred_element_type=F32
         )
-        a_t_rows = a_t_ref[rows, :].astype(F32)
-        pair_t_ref[0, rows, :] = a_t_rows
-        pair_t_ref[1, rows, :] = a_t_rows - jnp.dot(
-            a_t_ref[rows, :], g_t_ref[...], preferred_element_type=F32
-        )
+    transpose_into(pair_t_ref.at[0], pair_ref.at[0])
+    transpose_into(pair_t_ref.at[1], pair_ref.at[1])
 
 
 def filter_kernel(
-    flag_ref, prior_ref, w_ref, y_ref, a_ref, g_ref, a_t_ref, g_t_ref,
+    flag_ref, prior_ref, w_ref, y_ref, a_ref, g_ref,
     even_ref, odd_ref, extra_ref, prev_ref, pair_ref, pair_t_ref,
 ):
     half = y_ref.shape[1]
-    build_pairs(a_ref, g_ref, a_t_ref, g_t_ref, pair_ref, pair_t_ref)
+    build_pairs(a_ref, g_ref, pair_ref, pair_t_ref)
     gain = g_ref[...]
     transition = a_ref[...]
     w_even, w_odd = w_ref[0], w_ref[1]
@@ -98,7 +102,7 @@
 
 
 def smooth_kernel(
-    even_ref, odd_ref, a_ref, s_ref, s_t_ref,
+    even_ref, odd_ref, a_ref, s_ref,
     s_even_ref, s_odd_ref, extra_ref, d_even_ref, s32_ref, s32_t_ref,
 ):
     half = even_ref.shape[0]
@@ -106,7 +110,7 @@
     for start in range(0, width, BAND):
         rows = slice(start, start + BAND)
         s32_ref[rows, :] = s_ref[rows, :].astype(F32)
-        s32_t_ref[rows, :] = s_t_ref[rows, :].astype(F32)
+    transpose_into(s32_t_ref, s32_ref)
     smoother = s_ref[...]
     transition = a_ref[...]
     f_even, f_odd = even_ref[...], odd_ref[...]
@@ -146,19 +150,19 @@
     f_even, f_odd = pl.pallas_call(
         filter_kernel,
         out_shape=(rows, rows),
-        in_specs=[smem] + [vmem] * 7,
+        in_specs=[smem] + [vmem] * 5,
         out_specs=(vmem, vmem),
         scratch_shapes=[pltpu.VMEM((half, width), F32)] * 2 + [stacked, stacked],
         compiler_params=params,
-    )(flags, prior, w_pair, y_pair, transition, gain, transition.T, gain.T)
+    )(flags, prior, w_pair, y_pair, transition, gain)
     s_even, s_odd = pl.pallas_call(
         smooth_kernel,
         out_shape=(rows, rows),
-        in_specs=[vmem] * 5,
+        in_specs=[vmem] * 4,
         out_specs=(vmem, vmem),
         scratch_shapes=[pltpu.VMEM((half, width), F32)] * 2 + [square, square],
         compiler_params=params,
-    )(f_even, f_odd, transition, smoother, smoother.T)
+    )(f_even, f_odd, transition, smoother)
     interleave = lambda even, odd: jnp.stack([even, odd], axis=1).reshape(steps, width)
     return interleave(f_even, f_odd), interleave(s_even, s_odd)
 
@@ -211,12 +215,12 @@
 def local(prior, transition, gain, smoother, observed, present):
     panel = smoother.shape[0]
     seg, width = observed.shape
-    flags = jnp.broadcast_to(present.astype(F32)[:, None], (seg, 128))
-    block = jnp.concatenate([observed, flags], axis=1)
-    block = jnp.concatenate([block, jnp.zeros((8 - seg, width + 128), F32)], axis=0)
+    dense = seg * width // 128
+    flags = jnp.zeros((8, 128), F32).at[0, :seg].set(present.astype(F32))
+    block = jnp.concatenate([observed.reshape(dense, 128), flags], axis=0)
     slots = gather_over_time(block)
-    all_observed = slots[:, :seg, :width].reshape(-1, width)
-    weights = slots[:, :seg, width].reshape(-1)
+    all_observed = slots[:, :dense, :].reshape(-1, width)
+    weights = slots[:, dense, :seg].reshape(-1)
     smoother_full = lax.all_gather(smoother, "state", axis=0, tiled=True)
     filtered, smoothed = run_chain(
         weights, prior[None, :], transition, gain, smoother_full, all_observed

time: 183 us -> 156 us (0.85)
  Pallas kernels: 143 us -> 127 us
  local copies, waits for them, and re-layouts: 19 us -> 8.68 us
    pallas_call x1, Pallas kernels: 37.8 us -> 26 us  [gather_over_time(): pl.pallas_call(functools.partial(gather_kernel, count), out_shape=jax.Sha...]
    unnamed x4 -> x0, local copies, waits for them, and re-layouts: 6.55 us -> none
    all_gather x1 -> x0, local copies, waits for them, and re-layouts: 3.95 us -> none  [local(): smoother_full = lax.all_gather(smoother, 'state', axis=0, tiled=True)]
    pallas_call x1, Pallas kernels: 55.2 us -> 52.1 us  [run_chain(): pl.pallas_call(filter_kernel, out_shape=(rows, rows), in_specs=[smem] + [...]
  transfers between devices with their start and end apart: 1 -> 1, of which waited for: 0 -> 0; matrix products, arithmetic and copies ran while one was open for 10% -> 7% of each run, Pallas kernels for 51% -> 50%
where the time goes in v5:
time: 156 us; the launch traced here: 155 us
  Pallas kernels  127 us (81%)
  between operations  14.1 us (9%)
  local copies, waits for them, and re-layouts  8.68 us (6%)
  other arithmetic  4.36 us (3%)
    pallas_call x1, Pallas kernels, run_chain(): pl.pallas_call(filter_kernel, out_shape=(rows, rows), in_specs=[smem] + [...  52.1 us
    pallas_call x1, Pallas kernels, run_chain(): pl.pallas_call(smooth_kernel, out_shape=(rows, rows), in_specs=[vmem] * 4...  48.7 us
    pallas_call x1, Pallas kernels, gather_over_time(): pl.pallas_call(functools.partial(gather_kernel, count), out_shape=jax.Sha...  26 us
  transfers between devices with their start and end apart: 1, of which 0 were waited for; matrix products, arithmetic and copies ran while one was open for 7% of the time, Pallas kernels for 50%

profile of v5, /device:TPU:1, one launch (start us, length us, event | category | flops | bytes accessed | tf_op | source)
XLA Modules:
  0.0 154.6 jit_solution(2340107813207955237)
XLA Ops:
  7.2 0.0 all-gather.2.cloned.1.call-start
  7.2 0.7 all-gather.2.cloned.1.call-update
  7.9 0.7 reshape.44
  8.6 0.7 convert_bitcast_fusion
  9.3 0.6 select_maximum_fusion.block_ref
  9.9 26.0 %shard_map.77 = f32[32,40,128]{2,1,0:T(8,128)} custom-call(f32[40,128]{1,0:T(8,128)} %select_maximum_fusion.block_ref), custom_call_target="tpu_custom_call" | custom-call | tf_op jit(solution)/shard_map/pallas_call | solution.py:201
  35.9 1.1 slice.23
  37.0 0.3 reshape_reshape.3
  37.3 1.0 copy.18
  38.2 0.9 slice_reduce_fusion
  39.2 0.1 reshape_reshape_squeeze.3
  39.3 1.1 copy.12.w_ref
  40.4 1.0 convert_reduce_fusion
  41.3 0.6 convert_element_type.10.flag_ref
  42.0 52.1 %shard_map.78 = (f32[64,1024]{1,0:T(8,128)}, f32[64,1024]{1,0:T(8,128)}) custom-call(s32[128]{0:T(128)} %convert_element_type.10.flag_ref, f32[1,1024]{1,0:T(1,128)} %bitcast.19, f32[2,64,1]{2,1,0:T(8,128)} %copy.12.w_ref, f32[2,64,1024]{2,1,0:T(8,128)} %bitcast.13, bf16[1024,1024]{1,0:T(8,128)(2,1)} %a_ref.3, bf16[1024,1024]{1,0:T(8,128)(2,1)} %g_ref.1), custom_call_target="tpu_custom_call" | custom-call | tf_op jit(solution)/shard_map/pallas_call | solution.py:150
  94.0 1.1 pad_maximum_fusion
  95.1 0.4 copy.13
  95.5 0.4 reshape.46
  95.9 0.7 dynamic_slice.6
  96.6 0.0 all-gather.2.cloned.1.call-done.s_ref
  96.6 48.7 %shard_map.79 = (f32[64,1024]{1,0:T(8,128)}, f32[64,1024]{1,0:T(8,128)}) custom-call(f32[64,1024]{1,0:T(8,128)} %get-tuple-element.18.even_ref, f32[64,1024]{1,0:T(8,128)} %get-tuple-element.19.odd_ref, bf16[1024,1024]{1,0:T(8,128)(2,1)} %a_ref.3, bf16[1024,1024]{1,0:T(8,128)(2,1)} %all-gather.2.cloned.1.call-done.s_ref), custom_call_target="tpu_custom_call" | custom-call | tf_op jit(solution)/shard_map/pallas_call | solution.py:158
  145.2 1.1 pad_maximum_fusion.1
  146.3 0.4 copy.14
  146.7 0.4 reshape.47
  147.1 0.7 dynamic_slice.7
Async XLA Ops:
  7.2 89.4 %all-gather.2.cloned.1.call-start = ((), (), s32[]{:S(2)}) async-start(), calls=%async_computation | async-start | bytes 2228224 | tf_op jit(solution)/shard_map/all_gather | solution.py:224
Sparse Core Ops, SparseCore 0:
  10.1 48.9 all-gather.1

commit v6 on v5

--- a/solution.py
+++ b/solution.py
@@ -163,36 +163,72 @@
         scratch_shapes=[pltpu.VMEM((half, width), F32)] * 2 + [square, square],
         compiler_params=params,
     )(f_even, f_odd, transition, smoother)
-    interleave = lambda even, odd: jnp.stack([even, odd], axis=1).reshape(steps, width)
-    return interleave(f_even, f_odd), interleave(s_even, s_odd)
-
-
-def gather_kernel(count, block_ref, out_ref, local_sem, send_sems, recv_sems):
+    return (f_even, f_odd), (s_even, s_odd)
+
+
+def gather_kernel(count, block_ref, out_ref, local_sem, send_sems, recv_sems, swap_sems):
     me = lax.axis_index("tm")
+    lane = lax.axis_index("state")
+    core = lax.rem(lane, 2)
+    sibling = lane + 1 - 2 * core
+    half = count // 2
+    share = half - 1
     mesh_id = pl.DeviceIdType.MESH
     barrier = pltpu.get_barrier_semaphore()
     for step in range(1, count):
         peer = lax.rem(me + step, count)
         pl.semaphore_signal(barrier, inc=1, device_id={"tm": peer}, device_id_type=mesh_id)
-    pl.semaphore_wait(barrier, count - 1)
-    own = pltpu.make_async_copy(block_ref, out_ref.at[me], local_sem)
-    own.start()
-    copies = []
-    for step in range(1, count):
+    pl.semaphore_signal(barrier, inc=1, device_id={"state": sibling}, device_id_type=mesh_id)
+    pl.semaphore_wait(barrier, count)
+
+    def fetch(step):
         peer = lax.rem(me + step, count)
-        copy = pltpu.make_async_remote_copy(
+        return pltpu.make_async_remote_copy(
             src_ref=block_ref,
-            dst_ref=out_ref.at[me],
+            dst_ref=out_ref.at[step],
             send_sem=send_sems.at[step],
             recv_sem=recv_sems.at[step],
             device_id={"tm": peer},
             device_id_type=mesh_id,
         )
+
+    own = pltpu.make_async_copy(block_ref, out_ref.at[0], local_sem)
+
+    @pl.when(core == 0)
+    def _():
+        own.start()
+
+    copies = [fetch(core * share + j + 1) for j in range(share)]
+    for copy in copies:
         copy.start()
-        copies.append(copy)
+    last = fetch(count - 1)
+
+    @pl.when(core == 1)
+    def _():
+        last.start()
+
     for copy in copies:
         copy.wait()
-    own.wait()
+
+    @pl.when(core == 1)
+    def _():
+        last.wait()
+
+    @pl.when(core == 0)
+    def _():
+        own.wait()
+
+    mine = pl.ds(core * half, half)
+    swap = pltpu.make_async_remote_copy(
+        src_ref=out_ref.at[mine],
+        dst_ref=out_ref.at[mine],
+        send_sem=swap_sems.at[0],
+        recv_sem=swap_sems.at[1],
+        device_id={"state": sibling},
+        device_id_type=mesh_id,
+    )
+    swap.start()
+    swap.wait()
 
 
 def gather_over_time(block):
@@ -207,6 +243,7 @@
             pltpu.SemaphoreType.DMA,
             pltpu.SemaphoreType.DMA((count,)),
             pltpu.SemaphoreType.DMA((count,)),
+            pltpu.SemaphoreType.DMA((2,)),
         ],
         compiler_params=pltpu.CompilerParams(collective_id=0, has_side_effects=True),
     )(block)
@@ -215,20 +252,28 @@
 def local(prior, transition, gain, smoother, observed, present):
     panel = smoother.shape[0]
     seg, width = observed.shape
+    count = lax.axis_size("tm")
+    me = lax.axis_index("tm")
     dense = seg * width // 128
     flags = jnp.zeros((8, 128), F32).at[0, :seg].set(present.astype(F32))
     block = jnp.concatenate([observed.reshape(dense, 128), flags], axis=0)
     slots = gather_over_time(block)
+    order = lax.rem(me - jnp.arange(count) + count, count)
+    slots = jnp.take(slots, order, axis=0)
     all_observed = slots[:, :dense, :].reshape(-1, width)
     weights = slots[:, dense, :seg].reshape(-1)
     smoother_full = lax.all_gather(smoother, "state", axis=0, tiled=True)
-    filtered, smoothed = run_chain(
+    (f_even, f_odd), (s_even, s_odd) = run_chain(
         weights, prior[None, :], transition, gain, smoother_full, all_observed
     )
-    t0 = lax.axis_index("tm") * seg
+    r0 = me * (seg // 2)
     c0 = lax.axis_index("state") * panel
-    block_of = lambda full: lax.dynamic_slice(full, (t0, c0), (seg, panel))
-    return block_of(filtered), block_of(smoothed)
+
+    def block_of(even, odd):
+        pick = lambda rows: lax.dynamic_slice(rows, (r0, c0), (seg // 2, panel))
+        return jnp.stack([pick(even), pick(odd)], axis=1).reshape(seg, panel)
+
+    return block_of(f_even, f_odd), block_of(s_even, s_odd)
 
 
 def solution(mesh):

time: 156 us -> 151 us (0.968)
  other arithmetic: 4.36 us -> 1.47 us
    another operation x3, other arithmetic: 2.8 us -> 0.67 us  [the longest x2 2.14 us: run_chain(): jnp.stack([even, odd], axis=1).reshape(steps, width)]
    another operation x2 -> x4, local copies, waits for them, and re-layouts: 0.81 us -> 2.71 us  [block_of(): return jnp.stack([pick(even), pick(odd)], axis=1).reshape(seg, panel)]
    gather x0 -> x1, local copies, waits for them, and re-layouts: none -> 1.71 us  [local(): slots = jnp.take(slots, order, axis=0)]
  transfers between devices with their start and end apart: 1 -> 1, of which waited for: 0 -> 0; matrix products, arithmetic and copies ran while one was open for 7% -> 6% of each run, Pallas kernels for 50% -> 51%
where the time goes in v6:
time: 151 us
  Pallas kernels  126 us (83%)
  between operations  14.1 us (9%)
  local copies, waits for them, and re-layouts  8.29 us (5%)
    pallas_call x1, Pallas kernels, run_chain(): pl.pallas_call(filter_kernel, out_shape=(rows, rows), in_specs=[smem] + [...  52 us
    pallas_call x1, Pallas kernels, run_chain(): pl.pallas_call(smooth_kernel, out_shape=(rows, rows), in_specs=[vmem] * 4...  48.7 us
    pallas_call x1, Pallas kernels, gather_over_time(): pl.pallas_call(functools.partial(gather_kernel, count), out_shape=jax.Sha...  25.5 us
  transfers between devices with their start and end apart: 1, of which 0 were waited for; matrix products, arithmetic and copies ran while one was open for 6% of the time, Pallas kernels for 51%

profile of v6, /device:TPU:1, one launch (start us, length us, event | category | flops | bytes accessed | tf_op | source)
XLA Modules:
  0.0 150.8 jit_solution(14894727569031839086)
XLA Ops:
  7.2 0.0 all-gather.2.cloned.1.call-start
  7.2 0.7 all-gather.2.cloned.1.call-update
  7.9 0.7 reshape.86
  8.6 0.7 convert_bitcast_fusion
  9.3 0.6 select_maximum_fusion.block_ref
  9.9 25.5 %shard_map.77 = f32[32,40,128]{2,1,0:T(8,128)} custom-call(f32[40,128]{1,0:T(8,128)} %select_maximum_fusion.block_ref), custom_call_target="tpu_custom_call" | custom-call | tf_op jit(solution)/shard_map/pallas_call | solution.py:237
  35.4 1.7 %gather_fusion = f32[32,40,128]{2,1,0:T(8,128)S(1)} fusion(f32[32,40,128]{2,1,0:T(8,128)} %shard_map.77, s32[1024]{0:T(1024)S(1)} %pad_clamp_fusion), kind=kCustom, calls=%fused_computation | custom fusion | bytes 1310848 | tf_op jit(solution)/shard_map/jit(_take)/gather | solution.py:262
  37.1 0.1 broadcast_select_fusion
  37.3 0.1 slice.27
  37.3 0.3 reshape_reshape.3
  37.6 1.0 copy.18
  38.6 0.1 reshape_reshape_squeeze.3
  38.7 1.1 copy.12.w_ref
  39.8 0.1 convert_reduce_fusion
  39.9 0.6 convert_element_type.10.flag_ref
  40.5 52.0 %shard_map.78 = (f32[64,1024]{1,0:T(8,128)}, f32[64,1024]{1,0:T(8,128)}) custom-call(s32[128]{0:T(128)} %convert_element_type.10.flag_ref, f32[1,1024]{1,0:T(1,128)} %bitcast.23, f32[2,64,1]{2,1,0:T(8,128)} %copy.12.w_ref, f32[2,64,1024]{2,1,0:T(8,128)} %bitcast.21, bf16[1024,1024]{1,0:T(8,128)(2,1)} %a_ref.3, bf16[1024,1024]{1,0:T(8,128)(2,1)} %g_ref.1), custom_call_target="tpu_custom_call" | custom-call | tf_op jit(solution)/shard_map/pallas_call | solution.py:150
  92.5 0.8 dynamic-slice_bitcast_fusion.2
  93.3 0.6 copy.13
  93.9 0.0 all-gather.2.cloned.1.call-done.s_ref
  93.9 48.7 %shard_map.79 = (f32[64,1024]{1,0:T(8,128)}, f32[64,1024]{1,0:T(8,128)}) custom-call(f32[64,1024]{1,0:T(8,128)} %get-tuple-element.18.even_ref, f32[64,1024]{1,0:T(8,128)} %get-tuple-element.19.odd_ref, bf16[1024,1024]{1,0:T(8,128)(2,1)} %a_ref.3, bf16[1024,1024]{1,0:T(8,128)(2,1)} %all-gather.2.cloned.1.call-done.s_ref), custom_call_target="tpu_custom_call" | custom-call | tf_op jit(solution)/shard_map/pallas_call | solution.py:158
  142.6 0.8 dynamic-slice_bitcast_fusion
  143.4 0.6 copy.14
  (6 shorter events, 0.1 us)
Async XLA Ops:
  7.2 86.7 %all-gather.2.cloned.1.call-start = ((), (), s32[]{:S(2)}) async-start(), calls=%async_computation | async-start | bytes 2228224 | tf_op jit(solution)/shard_map/all_gather | solution.py:265
Sparse Core Ops, SparseCore 0:
  10.1 49.0 all-gather.1

commit v7 on v6

--- a/solution.py
+++ b/solution.py
@@ -21,11 +21,10 @@
 
 
 def times_transpose(rows, matrix):
-    total = None
-    for part in pieces(rows):
-        term = lax.dot_general(part, matrix, NT, preferred_element_type=F32)
-        total = term if total is None else total + term
-    return total
+    count = rows.shape[0]
+    stacked = jnp.concatenate(pieces(rows), axis=0)
+    out = lax.dot_general(stacked, matrix, NT, preferred_element_type=F32)
+    return out[0:count] + out[count : 2 * count] + out[2 * count :]
 
 
 def matvec_row(vector, matrix):
@@ -82,8 +81,9 @@
     transition = a_ref[...]
     w_even, w_odd = w_ref[0], w_ref[1]
     y_even, y_odd = y_ref[0], y_ref[1]
-    corr_even = w_even * times_transpose(y_even, gain)
-    corr_odd = w_odd * times_transpose(y_odd, gain)
+    both = times_transpose(jnp.concatenate([y_even, y_odd], axis=0), gain)
+    corr_even = w_even * both[:half]
+    corr_odd = w_odd * both[half:]
     moved = times_transpose(corr_even, transition)
     extra_ref[...] = moved - w_odd * times_transpose(moved, gain) + corr_odd
 
@@ -113,9 +113,10 @@
     transpose_into(s32_t_ref, s32_ref)
     smoother = s_ref[...]
     transition = a_ref[...]
-    f_even, f_odd = even_ref[...], odd_ref[...]
-    d_even_ref[...] = f_even - times_transpose(times_transpose(f_even, transition), smoother)
-    d_odd = f_odd - times_transpose(times_transpose(f_odd, transition), smoother)
+    both = jnp.concatenate([even_ref[...], odd_ref[...]], axis=0)
+    d_both = both - times_transpose(times_transpose(both, transition), smoother)
+    d_even_ref[...] = d_both[:half]
+    d_odd = d_both[half:]
     pulled = times_transpose(d_even_ref[...], smoother)
     extra_ref[0 : half - 1, :] = pulled[1:half, :] + d_odd[0 : half - 1, :]
     last = odd_ref[half - 1 : half, :]

time: 151 us -> 135 us (0.89)
  Pallas kernels: 126 us -> 110 us
    pallas_call x1, Pallas kernels: 48.7 us -> 40.5 us  [run_chain(): pl.pallas_call(smooth_kernel, out_shape=(rows, rows), in_specs=[vmem] * 4...]
    pallas_call x1, Pallas kernels: 52 us -> 44.1 us  [run_chain(): pl.pallas_call(filter_kernel, out_shape=(rows, rows), in_specs=[smem] + [...]
  transfers between devices with their start and end apart: 1 -> 1, of which waited for: 0 -> 0; matrix products, arithmetic and copies ran while one was open for 6% -> 6% of each run, Pallas kernels for 51% -> 52%
where the time goes in v7:
time: 135 us
  Pallas kernels  110 us (81%)
  between operations  14.1 us (10%)
  local copies, waits for them, and re-layouts  8.29 us (6%)
  other arithmetic  1.47 us (1%)
    pallas_call x1, Pallas kernels, run_chain(): pl.pallas_call(filter_kernel, out_shape=(rows, rows), in_specs=[smem] + [...  44.1 us
    pallas_call x1, Pallas kernels, run_chain(): pl.pallas_call(smooth_kernel, out_shape=(rows, rows), in_specs=[vmem] * 4...  40.5 us
    pallas_call x1, Pallas kernels, gather_over_time(): pl.pallas_call(functools.partial(gather_kernel, count), out_shape=jax.Sha...  25.5 us
    another operation x4, local copies, waits for them, and re-layouts, block_of(): return jnp.stack([pick(even), pick(odd)], axis=1).reshape(seg, panel)  2.71 us
  transfers between devices with their start and end apart: 1, of which 0 were waited for; matrix products, arithmetic and copies ran while one was open for 6% of the time, Pallas kernels for 52%

profile of v7, /device:TPU:1, one launch (start us, length us, event | category | flops | bytes accessed | tf_op | source)
XLA Modules:
  0.0 134.6 jit_solution(12771411458441873981)
XLA Ops:
  7.2 0.0 all-gather.2.cloned.1.call-start
  7.2 0.7 all-gather.2.cloned.1.call-update
  7.9 0.7 reshape.86
  8.6 0.7 convert_bitcast_fusion
  9.3 0.6 select_maximum_fusion.block_ref
  9.9 25.5 %shard_map.77 = f32[32,40,128]{2,1,0:T(8,128)} custom-call(f32[40,128]{1,0:T(8,128)} %select_maximum_fusion.block_ref), custom_call_target="tpu_custom_call" | custom-call | tf_op jit(solution)/shard_map/pallas_call | solution.py:238
  35.4 1.7 %gather_fusion = f32[32,40,128]{2,1,0:T(8,128)S(1)} fusion(f32[32,40,128]{2,1,0:T(8,128)} %shard_map.77, s32[1024]{0:T(1024)S(1)} %pad_clamp_fusion), kind=kCustom, calls=%fused_computation | custom fusion | bytes 1310848 | tf_op jit(solution)/shard_map/jit(_take)/gather | solution.py:263
  37.1 0.1 broadcast_select_fusion
  37.3 0.1 slice.27
  37.3 0.3 reshape_reshape.3
  37.6 1.0 copy.18
  38.6 0.1 reshape_reshape_squeeze.3
  38.7 1.1 copy.12.w_ref
  39.8 0.1 convert_reduce_fusion
  39.9 0.6 convert_element_type.10.flag_ref
  40.5 44.1 %shard_map.78 = (f32[64,1024]{1,0:T(8,128)}, f32[64,1024]{1,0:T(8,128)}) custom-call(s32[128]{0:T(128)} %convert_element_type.10.flag_ref, f32[1,1024]{1,0:T(1,128)} %bitcast.23, f32[2,64,1]{2,1,0:T(8,128)} %copy.12.w_ref, f32[2,64,1024]{2,1,0:T(8,128)} %bitcast.21, bf16[1024,1024]{1,0:T(8,128)(2,1)} %a_ref.3, bf16[1024,1024]{1,0:T(8,128)(2,1)} %g_ref.1), custom_call_target="tpu_custom_call" | custom-call | tf_op jit(solution)/shard_map/pallas_call | solution.py:151
  84.6 0.8 dynamic-slice_bitcast_fusion.2
  85.4 0.6 copy.13
  85.9 0.0 all-gather.2.cloned.1.call-done.s_ref
  85.9 40.5 %shard_map.79 = (f32[64,1024]{1,0:T(8,128)}, f32[64,1024]{1,0:T(8,128)}) custom-call(f32[64,1024]{1,0:T(8,128)} %get-tuple-element.18.even_ref, f32[64,1024]{1,0:T(8,128)} %get-tuple-element.19.odd_ref, bf16[1024,1024]{1,0:T(8,128)(2,1)} %a_ref.3, bf16[1024,1024]{1,0:T(8,128)(2,1)} %all-gather.2.cloned.1.call-done.s_ref), custom_call_target="tpu_custom_call" | custom-call | tf_op jit(solution)/shard_map/pallas_call | solution.py:159
  126.4 0.8 dynamic-slice_bitcast_fusion
  127.2 0.6 copy.14
  (6 shorter events, 0.1 us)
Async XLA Ops:
  7.2 78.8 %all-gather.2.cloned.1.call-start = ((), (), s32[]{:S(2)}) async-start(), calls=%async_computation | async-start | bytes 2228224 | tf_op jit(solution)/shard_map/all_gather | solution.py:266
Sparse Core Ops, SparseCore 0:
  10.1 49.0 all-gather.1

commit v8 on v7

--- a/solution.py
+++ b/solution.py
@@ -103,34 +103,45 @@
 
 def smooth_kernel(
     even_ref, odd_ref, a_ref, s_ref,
-    s_even_ref, s_odd_ref, extra_ref, d_even_ref, s32_ref, s32_t_ref,
+    s_even_ref, s_odd_ref, u_ref, v_ref, t_ref, sq_ref, sq_t_ref,
 ):
     half = even_ref.shape[0]
     width = s_ref.shape[0]
+    smoother = s_ref[...]
+    transition = a_ref[...]
     for start in range(0, width, BAND):
         rows = slice(start, start + BAND)
-        s32_ref[rows, :] = s_ref[rows, :].astype(F32)
-    transpose_into(s32_t_ref, s32_ref)
-    smoother = s_ref[...]
-    transition = a_ref[...]
+        sq_ref[rows, :] = jnp.dot(s_ref[rows, :], smoother, preferred_element_type=F32)
+    transpose_into(sq_t_ref, sq_ref)
     both = jnp.concatenate([even_ref[...], odd_ref[...]], axis=0)
     d_both = both - times_transpose(times_transpose(both, transition), smoother)
-    d_even_ref[...] = d_both[:half]
+    d_even = d_both[:half]
     d_odd = d_both[half:]
-    pulled = times_transpose(d_even_ref[...], smoother)
-    extra_ref[0 : half - 1, :] = pulled[1:half, :] + d_odd[0 : half - 1, :]
+    pulled = times_transpose(d_even, smoother)
+    u_ref[0:1, :] = jnp.zeros((1, width), F32)
+    u_ref[1:half, :] = pulled[1:half, :] + d_odd[0 : half - 1, :]
+    twice = times_transpose(times_transpose(u_ref[...], smoother), smoother)
+    v_ref[2:half, :] = twice[2:half, :] + u_ref[1 : half - 1, :]
+    s_odd_ref[...] = jnp.zeros((half, width), F32)
     last = odd_ref[half - 1 : half, :]
     s_odd_ref[half - 1 : half, :] = last
 
-    def pair_step(j, state):
-        r = half - 2 - j
-        middle = column_from_row(s32_ref[...], state)
-        value = row_from_column(s32_t_ref[...], middle) + extra_ref[pl.ds(r, 1), :]
-        s_odd_ref[pl.ds(r, 1), :] = value
+    def quad_step(j, state):
+        q = half - 1 - 2 * j
+        middle = column_from_row(sq_ref[...], state)
+        value = row_from_column(sq_t_ref[...], middle) + v_ref[pl.ds(q, 1), :]
+        s_odd_ref[pl.ds(q - 2, 1), :] = value
         return value
 
-    lax.fori_loop(0, half - 1, pair_step, last)
-    s_even_ref[...] = times_transpose(s_odd_ref[...], smoother) + d_even_ref[...]
+    lax.fori_loop(0, half // 2 - 1, quad_step, last)
+    odd_row = lax.broadcasted_iota(jnp.int32, (half, 1), 0) % 2 == 1
+    first = times_transpose(s_odd_ref[...], smoother) + d_even
+    s_even_ref[...] = jnp.where(odd_row, first, 0.0)
+    t_ref[...] = times_transpose(s_even_ref[...], smoother)
+    filled = t_ref[1:half, :] + d_odd[0 : half - 1, :]
+    s_odd_ref[0 : half - 1, :] = jnp.where(odd_row[0 : half - 1], s_odd_ref[0 : half - 1, :], filled)
+    third = times_transpose(s_odd_ref[...], smoother) + d_even
+    s_even_ref[...] = jnp.where(odd_row, s_even_ref[...], third)
 
 
 VMEM_LIMIT = 60 * 1024 * 1024
@@ -161,7 +172,7 @@
         out_shape=(rows, rows),
         in_specs=[vmem] * 4,
         out_specs=(vmem, vmem),
-        scratch_shapes=[pltpu.VMEM((half, width), F32)] * 2 + [square, square],
+        scratch_shapes=[pltpu.VMEM((half, width), F32)] * 3 + [square, square],
         compiler_params=params,
     )(f_even, f_odd, transition, smoother)
     return (f_even, f_odd), (s_even, s_odd)

time: 135 us -> 123 us (0.911)
  Pallas kernels: 110 us -> 97.8 us
    pallas_call x1, Pallas kernels: 40.5 us -> 28 us  [run_chain(): pl.pallas_call(smooth_kernel, out_shape=(rows, rows), in_specs=[vmem] * 4...]
  transfers between devices with their start and end apart: 1 -> 1, of which waited for: 0 -> 0; matrix products, arithmetic and copies ran while one was open for 6% -> 7% of each run, Pallas kernels for 52% -> 57%
where the time goes in v8:
time: 123 us; the launch traced here: 122 us
  Pallas kernels  97.8 us (80%)
  between operations  14.1 us (11%)
  local copies, waits for them, and re-layouts  8.29 us (7%)
  other arithmetic  1.47 us (1%)
    pallas_call x1, Pallas kernels, run_chain(): pl.pallas_call(filter_kernel, out_shape=(rows, rows), in_specs=[smem] + [...  44.3 us
    pallas_call x1, Pallas kernels, run_chain(): pl.pallas_call(smooth_kernel, out_shape=(rows, rows), in_specs=[vmem] * 4...  28 us
    pallas_call x1, Pallas kernels, gather_over_time(): pl.pallas_call(functools.partial(gather_kernel, count), out_shape=jax.Sha...  25.5 us
    another operation x4, local copies, waits for them, and re-layouts, block_of(): return jnp.stack([pick(even), pick(odd)], axis=1).reshape(seg, panel)  2.71 us
  transfers between devices with their start and end apart: 1, of which 0 were waited for; matrix products, arithmetic and copies ran while one was open for 7% of the time, Pallas kernels for 57%

profile of v8, /device:TPU:1, one launch (start us, length us, event | category | flops | bytes accessed | tf_op | source)
XLA Modules:
  0.0 122.4 jit_solution(1225845274577116923)
XLA Ops:
  7.2 0.0 all-gather.2.cloned.1.call-start
  7.2 0.7 all-gather.2.cloned.1.call-update
  7.9 0.7 reshape.86
  8.6 0.7 convert_bitcast_fusion
  9.3 0.6 select_maximum_fusion.block_ref
  9.9 25.5 %shard_map.77 = f32[32,40,128]{2,1,0:T(8,128)} custom-call(f32[40,128]{1,0:T(8,128)} %select_maximum_fusion.block_ref), custom_call_target="tpu_custom_call" | custom-call | tf_op jit(solution)/shard_map/pallas_call | solution.py:249
  35.4 1.7 %gather_fusion = f32[32,40,128]{2,1,0:T(8,128)S(1)} fusion(f32[32,40,128]{2,1,0:T(8,128)} %shard_map.77, s32[1024]{0:T(1024)S(1)} %pad_clamp_fusion), kind=kCustom, calls=%fused_computation | custom fusion | bytes 1310848 | tf_op jit(solution)/shard_map/jit(_take)/gather | solution.py:274
  37.1 0.1 broadcast_select_fusion
  37.3 0.1 slice.27
  37.3 0.3 reshape_reshape.3
  37.6 1.0 copy.18
  38.6 0.1 reshape_reshape_squeeze.3
  38.7 1.1 copy.12.w_ref
  39.8 0.1 convert_reduce_fusion
  39.9 0.6 convert_element_type.10.flag_ref
  40.5 44.3 %shard_map.78 = (f32[64,1024]{1,0:T(8,128)}, f32[64,1024]{1,0:T(8,128)}) custom-call(s32[128]{0:T(128)} %convert_element_type.10.flag_ref, f32[1,1024]{1,0:T(1,128)} %bitcast.23, f32[2,64,1]{2,1,0:T(8,128)} %copy.12.w_ref, f32[2,64,1024]{2,1,0:T(8,128)} %bitcast.21, bf16[1024,1024]{1,0:T(8,128)(2,1)} %a_ref.3, bf16[1024,1024]{1,0:T(8,128)(2,1)} %g_ref.1), custom_call_target="tpu_custom_call" | custom-call | tf_op jit(solution)/shard_map/pallas_call | solution.py:162
  84.8 0.8 dynamic-slice_bitcast_fusion.2
  85.6 0.6 copy.13
  86.1 0.0 all-gather.2.cloned.1.call-done.s_ref
  86.1 28.0 %shard_map.79 = (f32[64,1024]{1,0:T(8,128)}, f32[64,1024]{1,0:T(8,128)}) custom-call(f32[64,1024]{1,0:T(8,128)} %get-tuple-element.18.even_ref, f32[64,1024]{1,0:T(8,128)} %get-tuple-element.19.odd_ref, bf16[1024,1024]{1,0:T(8,128)(2,1)} %a_ref.3, bf16[1024,1024]{1,0:T(8,128)(2,1)} %all-gather.2.cloned.1.call-done.s_ref), custom_call_target="tpu_custom_call" | custom-call | tf_op jit(solution)/shard_map/pallas_call | solution.py:170
  114.2 0.8 dynamic-slice_bitcast_fusion
  114.9 0.6 copy.14
  (6 shorter events, 0.1 us)
Async XLA Ops:
  7.2 79.0 %all-gather.2.cloned.1.call-start = ((), (), s32[]{:S(2)}) async-start(), calls=%async_computation | async-start | bytes 2228224 | tf_op jit(solution)/shard_map/all_gather | solution.py:277
Sparse Core Ops, SparseCore 0:
  10.1 49.0 all-gather.1

commit v9 on v8

--- a/solution.py
+++ b/solution.py
@@ -261,6 +261,29 @@
     )(block)
 
 
+def shifted(block, axis, count, distance):
+    return lax.ppermute(block, axis, [(i, (i + distance) % count) for i in range(count)])
+
+
+def gather_over_state(panel, tied):
+    count = lax.axis_size("state")
+    me = lax.axis_index("state")
+    group = 1
+    while group * group < count:
+        group += 1
+    if group * group != count:
+        group = count
+    first = jnp.stack([panel] + [shifted(panel, "state", count, d) for d in range(1, group)])
+    first, tied = lax.optimization_barrier((first, tied))
+    rounds = [first] + [
+        shifted(first, "state", count, group * q) for q in range(1, count // group)
+    ]
+    stacked = jnp.concatenate(rounds, axis=0)
+    order = lax.rem(me - jnp.arange(count) + count, count)
+    stacked = jnp.take(stacked, order, axis=0)
+    return stacked.reshape(count * panel.shape[0], panel.shape[1]), tied
+
+
 def local(prior, transition, gain, smoother, observed, present):
     panel = smoother.shape[0]
     seg, width = observed.shape
@@ -274,7 +297,7 @@
     slots = jnp.take(slots, order, axis=0)
     all_observed = slots[:, :dense, :].reshape(-1, width)
     weights = slots[:, dense, :seg].reshape(-1)
-    smoother_full = lax.all_gather(smoother, "state", axis=0, tiled=True)
+    smoother_full, all_observed = gather_over_state(smoother, all_observed)
     (f_even, f_odd), (s_even, s_odd) = run_chain(
         weights, prior[None, :], transition, gain, smoother_full, all_observed
     )

time: 123 us -> 136 us (1.11)
  starting transfers between devices: 0.04 us -> 25.6 us
  between operations: 14.1 us -> 0.81 us
  Pallas kernels: 97.8 us -> 92.9 us
  other arithmetic: 1.47 us -> 4.91 us
  local copies, waits for them, and re-layouts: 8.29 us -> 10.8 us
    ppermute x0 -> x6, starting transfers between devices: none -> 25.6 us  [shifted(): lax.ppermute(block, axis, [(i, (i + distance) % count) for i in range(cou...]
    pallas_call x1, Pallas kernels: 25.5 us -> 20.7 us  [gather_over_time(): pl.pallas_call(functools.partial(gather_kernel, count), out_shape=jax.Sha...]
    gather x0 -> x1, local copies, waits for them, and re-layouts: none -> 2.27 us  [gather_over_state(): stacked = jnp.take(stacked, order, axis=0)]
    select_n x0 -> x2, other arithmetic: none -> 1.74 us  [gather_over_state(): stacked = jnp.take(stacked, order, axis=0)]
    concatenate x0 -> x1, other arithmetic: none -> 1.6 us  [gather_over_state(): stacked = jnp.concatenate(rounds, axis=0)]
  transfers between devices with their start and end apart: 1 -> 6, of which waited for: 0 -> 0; matrix products, arithmetic and copies ran while one was open for 7% -> 6% of each run, Pallas kernels for 57% -> 48%
where the time goes in v9:
time: 136 us; the launch traced here: 135 us
  Pallas kernels  92.9 us (68%)
  starting transfers between devices  25.6 us (19%)
  local copies, waits for them, and re-layouts  10.8 us (8%)
  other arithmetic  4.91 us (4%)
    pallas_call x1, Pallas kernels, run_chain(): pl.pallas_call(filter_kernel, out_shape=(rows, rows), in_specs=[smem] + [...  44.3 us
    pallas_call x1, Pallas kernels, run_chain(): pl.pallas_call(smooth_kernel, out_shape=(rows, rows), in_specs=[vmem] * 4...  28 us
    ppermute x6, starting transfers between devices, shifted(): lax.ppermute(block, axis, [(i, (i + distance) % count) for i in range(cou...  25.6 us
    pallas_call x1, Pallas kernels, gather_over_time(): pl.pallas_call(functools.partial(gather_kernel, count), out_shape=jax.Sha...  20.7 us
  transfers between devices with their start and end apart: 6, of which 0 were waited for; matrix products, arithmetic and copies ran while one was open for 6% of the time, Pallas kernels for 48%

profile of v9, /device:TPU:1, one launch (start us, length us, event | category | flops | bytes accessed | tf_op | source)
XLA Modules:
  0.0 135.1 jit_solution(15687035313427385455)
XLA Ops:
  0.6 7.2 %collective-permute-start.2 = (bf16[64,1024]{1,0:T(8,128)(2,1)}, bf16[64,1024]{1,0:T(8,128)(2,1)S(1)}, u32[]{:S(2)}, u32[]{:S(2)}) collective-permute-start(bf16[64,1024]{1,0:T(8,128)(2,1)} %param.11), channel_id=1, source_target_pairs={{0,3},{1,4},{2,5},{3,6},{4,7},{5,8},{6,9},{7,10},{8,11},{9,12},{10... | collective-permute-start | bytes 393224 | tf_op jit(solution)/shard_map/ppermute | solution.py:265
  7.8 4.0 %collective-permute-start.1 = (bf16[64,1024]{1,0:T(8,128)(2,1)}, bf16[64,1024]{1,0:T(8,128)(2,1)S(1)}, u32[]{:S(2)}, u32[]{:S(2)}) collective-permute-start(bf16[64,1024]{1,0:T(8,128)(2,1)} %param.11), channel_id=1, source_target_pairs={{0,2},{1,3},{2,4},{3,5},{4,6},{5,7},{6,8},{7,9},{8,10},{9,11},{10,... | collective-permute-start | bytes 393224 | tf_op jit(solution)/shard_map/ppermute | solution.py:265
  11.8 0.3 collective-permute-start
  12.2 0.7 convert_bitcast_fusion
  12.8 0.7 reshape.137
  13.6 0.6 select_maximum_fusion.block_ref
  14.2 20.7 %shard_map.77 = f32[32,40,128]{2,1,0:T(8,128)} custom-call(f32[40,128]{1,0:T(8,128)} %select_maximum_fusion.block_ref), custom_call_target="tpu_custom_call" | custom-call | tf_op jit(solution)/shard_map/pallas_call | solution.py:249
  34.9 1.7 %gather_fusion = f32[32,40,128]{2,1,0:T(8,128)S(1)} fusion(f32[32,40,128]{2,1,0:T(8,128)} %shard_map.77, s32[1024]{0:T(1024)S(1)} %pad_clamp_fusion.1), kind=kCustom, calls=%fused_computation | custom fusion | bytes 1310848 | tf_op jit(solution)/shard_map/jit(_take)/gather | solution.py:297
  36.6 0.1 broadcast_select_fusion
  36.7 0.1 convert_reduce_fusion
  36.8 0.1 slice.29
  36.8 0.6 convert_element_type.10.flag_ref
  37.5 0.1 reshape_reshape_squeeze.3
  37.6 1.1 copy.12.w_ref
  38.7 0.1 reshape.139
  38.8 0.1 pad_maximum_fusion.1
  38.9 5.6 %collective-permute-start.5 = (bf16[4,64,1024]{2,1,0:T(8,128)(2,1)S(1)}, bf16[4,64,1024]{2,1,0:T(8,128)(2,1)S(1)}, u32[]{:S(2)}, u32[]{:S(2)}) collective-permute-start(bf16[4,64,1024]{2,1,0:T(8,128)(2,1)S(1)} %pad_maximum_fusion.1), channel_id=1, source_target_pairs={{0,12},{1,13},{2,14},{3,15},{4,0},{5,1},{6,2},{7,3},{8,4},{9,5},{1... | collective-permute-start | bytes 1572872 | tf_op jit(solution)/shard_map/ppermute | solution.py:265
  44.5 5.7 %collective-permute-start.4 = (bf16[4,64,1024]{2,1,0:T(8,128)(2,1)S(1)}, bf16[4,64,1024]{2,1,0:T(8,128)(2,1)S(1)}, u32[]{:S(2)}, u32[]{:S(2)}) collective-permute-start(bf16[4,64,1024]{2,1,0:T(8,128)(2,1)S(1)} %pad_maximum_fusion.1), channel_id=1, source_target_pairs={{0,8},{1,9},{2,10},{3,11},{4,12},{5,13},{6,14},{7,15},{8,0},{9,1},... | collective-permute-start | bytes 1572872 | tf_op jit(solution)/shard_map/ppermute | solution.py:265
  50.2 2.8 %collective-permute-start.3 = (bf16[4,64,1024]{2,1,0:T(8,128)(2,1)S(1)}, bf16[4,64,1024]{2,1,0:T(8,128)(2,1)S(1)}, u32[]{:S(2)}, u32[]{:S(2)}) collective-permute-start(bf16[4,64,1024]{2,1,0:T(8,128)(2,1)S(1)} %pad_maximum_fusion.1), channel_id=1, source_target_pairs={{0,4},{1,5},{2,6},{3,7},{4,8},{5,9},{6,10},{7,11},{8,12},{9,13},{1... | collective-permute-start | bytes 1572872 | tf_op jit(solution)/shard_map/ppermute | solution.py:265
  53.1 0.1 broadcast_in_dim.35
  53.1 0.1 broadcast_in_dim.36
  53.2 0.3 reshape.140
  53.6 0.9 copy.18
  54.5 44.3 %shard_map.78 = (f32[64,1024]{1,0:T(8,128)}, f32[64,1024]{1,0:T(8,128)}) custom-call(s32[128]{0:T(128)} %convert_element_type.10.flag_ref, f32[1,1024]{1,0:T(1,128)} %bitcast.35, f32[2,64,1]{2,1,0:T(8,128)} %copy.12.w_ref, f32[2,64,1024]{2,1,0:T(8,128)} %bitcast.29, bf16[1024,1024]{1,0:T(8,128)(2,1)} %a_ref.3, bf16[1024,1024]{1,0:T(8,128)(2,1)} %g_ref.1), custom_call_target="tpu_custom_call" | custom-call | tf_op jit(solution)/shard_map/pallas_call | solution.py:162
  98.8 0.8 dynamic-slice_bitcast_fusion.2
  99.5 0.6 copy.13
  100.1 1.6 %pad_maximum_fusion = bf16[16,64,1024]{2,1,0:T(8,128)(2,1)} fusion(bf16[4,64,1024]{2,1,0:T(8,128)(2,1)S(1)} %collective-permute-done.5, bf16[4,64,1024]{2,1,0:T(8,128)(2,1)S(1)} %collective-permute-done.4, bf16[4,64,1024]{2,1,0:T(8,128)(2,1)S(1)} %collective-permute-done.3, bf16[4,64,1024]{2,1,0:T(8,128)(2,1)S(1)} %pad_maximum_fusion.1), kind=kLoop, calls=%fused_computation.2 | loop fusion | flops 3145728 | bytes 4194304 | tf_op jit(solution)/shard_map/concatenate | solution.py:281
  101.7 2.3 %gather_fusion.1 = bf16[16,64,1024]{2,1,0:T(8,128)(2,1)S(1)} fusion(bf16[16,64,1024]{2,1,0:T(8,128)(2,1)} %pad_maximum_fusion, s32[1024]{0:T(1024)S(1)} %pad_clamp_fusion), kind=kCustom, calls=%fused_computation.1 | custom fusion | bytes 4194368 | tf_op jit(solution)/shard_map/jit(_take)/gather | solution.py:283
  104.0 1.7 %bitcast_select_fusion.s_ref = bf16[1024,1024]{1,0:T(8,128)(2,1)} fusion(bf16[16,64,1024]{2,1,0:T(8,128)(2,1)S(1)} %gather_fusion.1, pred[1024]{0:T(1024)(128)(4,1)S(1)} %broadcast_in_dim.36), kind=kLoop, calls=%fused_computation.3 | loop fusion | flops 1048576 | bytes 4195328 | tf_op jit(solution)/shard_map/jit(_take)/select_n | solution.py:283
  105.7 28.0 %shard_map.79 = (f32[64,1024]{1,0:T(8,128)}, f32[64,1024]{1,0:T(8,128)}) custom-call(f32[64,1024]{1,0:T(8,128)} %get-tuple-element.21.even_ref, f32[64,1024]{1,0:T(8,128)} %get-tuple-element.22.odd_ref, bf16[1024,1024]{1,0:T(8,128)(2,1)} %a_ref.3, bf16[1024,1024]{1,0:T(8,128)(2,1)} %bitcast_select_fusion.s_ref), custom_call_target="tpu_custom_call" | custom-call | tf_op jit(solution)/shard_map/pallas_call | solution.py:170
  133.7 0.8 dynamic-slice_bitcast_fusion
  134.5 0.6 copy.14
  (17 shorter events, 0.1 us)
Async XLA Ops:
  0.6 38.1 %collective-permute-start.2 = (bf16[64,1024]{1,0:T(8,128)(2,1)}, bf16[64,1024]{1,0:T(8,128)(2,1)S(1)}, u32[]{:S(2)}, u32[]{:S(2)}) collective-permute-start(bf16[64,1024]{1,0:T(8,128)(2,1)} %param.11), channel_id=1, source_target_pairs={{0,3},{1,4},{2,5},{3,6},{4,7},{5,8},{6,9},{7,10},{8,11},{9,12},{10... | collective-permute-start | bytes 393224 | tf_op jit(solution)/shard_map/ppermute | solution.py:265
  7.8 30.9 %collective-permute-start.1 = (bf16[64,1024]{1,0:T(8,128)(2,1)}, bf16[64,1024]{1,0:T(8,128)(2,1)S(1)}, u32[]{:S(2)}, u32[]{:S(2)}) collective-permute-start(bf16[64,1024]{1,0:T(8,128)(2,1)} %param.11), channel_id=1, source_target_pairs={{0,2},{1,3},{2,4},{3,5},{4,6},{5,7},{6,8},{7,9},{8,10},{9,11},{10,... | collective-permute-start | bytes 393224 | tf_op jit(solution)/shard_map/ppermute | solution.py:265
  11.8 26.9 %collective-permute-start = (bf16[64,1024]{1,0:T(8,128)(2,1)}, bf16[64,1024]{1,0:T(8,128)(2,1)S(1)}, u32[]{:S(2)}, u32[]{:S(2)}) collective-permute-start(bf16[64,1024]{1,0:T(8,128)(2,1)} %param.11), channel_id=1, source_target_pairs={{0,1},{1,2},{2,3},{3,4},{4,5},{5,6},{6,7},{7,8},{8,9},{9,10},{10,1... | collective-permute-start | bytes 393224 | tf_op jit(solution)/shard_map/ppermute | solution.py:265
  36.6 2.2 %copy-start = (bf16[64,1024]{1,0:T(8,128)(2,1)S(1)}, bf16[64,1024]{1,0:T(8,128)(2,1)}, u32[]{:S(2)}) copy-start(bf16[64,1024]{1,0:T(8,128)(2,1)} %param.11) | copy-start | bytes 393220
  38.9 61.2 %collective-permute-start.5 = (bf16[4,64,1024]{2,1,0:T(8,128)(2,1)S(1)}, bf16[4,64,1024]{2,1,0:T(8,128)(2,1)S(1)}, u32[]{:S(2)}, u32[]{:S(2)}) collective-permute-start(bf16[4,64,1024]{2,1,0:T(8,128)(2,1)S(1)} %pad_maximum_fusion.1), channel_id=1, source_target_pairs={{0,12},{1,13},{2,14},{3,15},{4,0},{5,1},{6,2},{7,3},{8,4},{9,5},{1... | collective-permute-start | bytes 1572872 | tf_op jit(solution)/shard_map/ppermute | solution.py:265
  44.5 55.6 %collective-permute-start.4 = (bf16[4,64,1024]{2,1,0:T(8,128)(2,1)S(1)}, bf16[4,64,1024]{2,1,0:T(8,128)(2,1)S(1)}, u32[]{:S(2)}, u32[]{:S(2)}) collective-permute-start(bf16[4,64,1024]{2,1,0:T(8,128)(2,1)S(1)} %pad_maximum_fusion.1), channel_id=1, source_target_pairs={{0,8},{1,9},{2,10},{3,11},{4,12},{5,13},{6,14},{7,15},{8,0},{9,1},... | collective-permute-start | bytes 1572872 | tf_op jit(solution)/shard_map/ppermute | solution.py:265
  50.2 49.9 %collective-permute-start.3 = (bf16[4,64,1024]{2,1,0:T(8,128)(2,1)S(1)}, bf16[4,64,1024]{2,1,0:T(8,128)(2,1)S(1)}, u32[]{:S(2)}, u32[]{:S(2)}) collective-permute-start(bf16[4,64,1024]{2,1,0:T(8,128)(2,1)S(1)} %pad_maximum_fusion.1), channel_id=1, source_target_pairs={{0,4},{1,5},{2,6},{3,7},{4,8},{5,9},{6,10},{7,11},{8,12},{9,13},{1... | collective-permute-start | bytes 1572872 | tf_op jit(solution)/shard_map/ppermute | solution.py:265

commit v10 on v8

--- a/solution.py
+++ b/solution.py
@@ -71,9 +71,17 @@
     transpose_into(pair_t_ref.at[1], pair_ref.at[1])
 
 
+def own_rows(even_ref, odd_ref, out_ref):
+    per = out_ref.shape[0] // 2
+    base = lax.axis_index("tm") * per
+    for i in range(per):
+        out_ref[2 * i : 2 * i + 1, :] = even_ref[pl.ds(base + i, 1), :]
+        out_ref[2 * i + 1 : 2 * i + 2, :] = odd_ref[pl.ds(base + i, 1), :]
+
+
 def filter_kernel(
     flag_ref, prior_ref, w_ref, y_ref, a_ref, g_ref,
-    even_ref, odd_ref, extra_ref, prev_ref, pair_ref, pair_t_ref,
+    even_ref, odd_ref, own_ref, extra_ref, prev_ref, pair_ref, pair_t_ref,
 ):
     half = y_ref.shape[1]
     build_pairs(a_ref, g_ref, pair_ref, pair_t_ref)
@@ -99,11 +107,12 @@
     prev_ref[1:half, :] = odd_ref[0 : half - 1, :]
     predicted = times_transpose(prev_ref[...], transition)
     even_ref[...] = predicted + w_even * times_transpose(y_even - predicted, gain)
+    own_rows(even_ref, odd_ref, own_ref)
 
 
 def smooth_kernel(
     even_ref, odd_ref, a_ref, s_ref,
-    s_even_ref, s_odd_ref, u_ref, v_ref, t_ref, sq_ref, sq_t_ref,
+    s_even_ref, s_odd_ref, own_ref, u_ref, v_ref, t_ref, sq_ref, sq_t_ref,
 ):
     half = even_ref.shape[0]
     width = s_ref.shape[0]
@@ -142,6 +151,7 @@
     s_odd_ref[0 : half - 1, :] = jnp.where(odd_row[0 : half - 1], s_odd_ref[0 : half - 1, :], filled)
     third = times_transpose(s_odd_ref[...], smoother) + d_even
     s_even_ref[...] = jnp.where(odd_row, s_even_ref[...], third)
+    own_rows(s_even_ref, s_odd_ref, own_ref)
 
 
 VMEM_LIMIT = 60 * 1024 * 1024
@@ -159,23 +169,25 @@
     rows = jax.ShapeDtypeStruct((half, width), F32)
     square = pltpu.VMEM((width, width), F32)
     stacked = pltpu.VMEM((2, width, width), F32)
-    f_even, f_odd = pl.pallas_call(
+    seg = steps // lax.axis_size("tm")
+    own = jax.ShapeDtypeStruct((seg, width), F32)
+    f_even, f_odd, f_own = pl.pallas_call(
         filter_kernel,
-        out_shape=(rows, rows),
+        out_shape=(rows, rows, own),
         in_specs=[smem] + [vmem] * 5,
-        out_specs=(vmem, vmem),
+        out_specs=(vmem, vmem, vmem),
         scratch_shapes=[pltpu.VMEM((half, width), F32)] * 2 + [stacked, stacked],
         compiler_params=params,
     )(flags, prior, w_pair, y_pair, transition, gain)
-    s_even, s_odd = pl.pallas_call(
+    _, _, s_own = pl.pallas_call(
         smooth_kernel,
-        out_shape=(rows, rows),
+        out_shape=(rows, rows, own),
         in_specs=[vmem] * 4,
-        out_specs=(vmem, vmem),
+        out_specs=(vmem, vmem, vmem),
         scratch_shapes=[pltpu.VMEM((half, width), F32)] * 3 + [square, square],
         compiler_params=params,
     )(f_even, f_odd, transition, smoother)
-    return (f_even, f_odd), (s_even, s_odd)
+    return f_own, s_own
 
 
 def gather_kernel(count, block_ref, out_ref, local_sem, send_sems, recv_sems, swap_sems):
@@ -275,17 +287,12 @@
     all_observed = slots[:, :dense, :].reshape(-1, width)
     weights = slots[:, dense, :seg].reshape(-1)
     smoother_full = lax.all_gather(smoother, "state", axis=0, tiled=True)
-    (f_even, f_odd), (s_even, s_odd) = run_chain(
+    f_own, s_own = run_chain(
         weights, prior[None, :], transition, gain, smoother_full, all_observed
     )
-    r0 = me * (seg // 2)
     c0 = lax.axis_index("state") * panel
-
-    def block_of(even, odd):
-        pick = lambda rows: lax.dynamic_slice(rows, (r0, c0), (seg // 2, panel))
-        return jnp.stack([pick(even), pick(odd)], axis=1).reshape(seg, panel)
-
-    return block_of(f_even, f_odd), block_of(s_even, s_odd)
+    block_of = lambda rows: lax.dynamic_slice_in_dim(rows, c0, panel, 1)
+    return block_of(f_own), block_of(s_own)
 
 
 def solution(mesh):

time: 123 us -> 123 us (level)
    another operation x4 -> x0, local copies, waits for them, and re-layouts: 2.71 us -> none  [block_of(): return jnp.stack([pick(even), pick(odd)], axis=1).reshape(seg, panel)]
    dynamic_slice x0 -> x2, local copies, waits for them, and re-layouts: none -> 2.65 us  [local(): block_of = lambda rows: lax.dynamic_slice_in_dim(rows, c0, panel, 1)]
where the time goes in v10:
time: 123 us; the launch traced here: 122 us
  Pallas kernels  97.8 us (80%)
  between operations  14.1 us (11%)
  local copies, waits for them, and re-layouts  8.23 us (7%)
  other arithmetic  1.46 us (1%)
    pallas_call x1, Pallas kernels, run_chain(): pl.pallas_call(filter_kernel, out_shape=(rows, rows, own), in_specs=[smem...  44.3 us
    pallas_call x1, Pallas kernels, run_chain(): pl.pallas_call(smooth_kernel, out_shape=(rows, rows, own), in_specs=[vmem...  28 us
    pallas_call x1, Pallas kernels, gather_over_time(): pl.pallas_call(functools.partial(gather_kernel, count), out_shape=jax.Sha...  25.5 us
    dynamic_slice x2, local copies, waits for them, and re-layouts, local(): block_of = lambda rows: lax.dynamic_slice_in_dim(rows, c0, panel, 1)  2.65 us
  transfers between devices with their start and end apart: 1, of which 0 were waited for; matrix products, arithmetic and copies ran while one was open for 7% of the time, Pallas kernels for 57%

profile of v10, /device:TPU:1, one launch (start us, length us, event | category | flops | bytes accessed | tf_op | source)
XLA Modules:
  0.0 122.3 jit_solution(15391911488430307263)
XLA Ops:
  7.2 0.0 all-gather.2.cloned.1.call-start
  7.2 0.7 all-gather.2.cloned.1.call-update
  7.9 0.7 reshape.80
  8.6 0.7 convert_bitcast_fusion
  9.3 0.6 select_maximum_fusion.block_ref
  9.9 25.5 %shard_map.77 = f32[32,40,128]{2,1,0:T(8,128)} custom-call(f32[40,128]{1,0:T(8,128)} %select_maximum_fusion.block_ref), custom_call_target="tpu_custom_call" | custom-call | tf_op jit(solution)/shard_map/pallas_call | solution.py:261
  35.4 1.7 %gather_fusion = f32[32,40,128]{2,1,0:T(8,128)S(1)} fusion(f32[32,40,128]{2,1,0:T(8,128)} %shard_map.77, s32[1024]{0:T(1024)S(1)} %pad_clamp_fusion), kind=kCustom, calls=%fused_computation | custom fusion | bytes 1310848 | tf_op jit(solution)/shard_map/jit(_take)/gather | solution.py:286
  37.1 0.1 broadcast_select_fusion
  37.3 0.1 slice.27
  37.3 0.1 convert_reduce_fusion
  37.4 0.6 convert_element_type.10.flag_ref
  38.0 0.1 reshape_reshape_squeeze.3
  38.1 1.1 copy.12.w_ref
  39.2 0.3 reshape_reshape.3
  39.5 1.0 copy.16
  40.5 44.3 %shard_map.78 = (f32[64,1024]{1,0:T(8,128)}, f32[64,1024]{1,0:T(8,128)}, f32[4,1024]{1,0:T(4,128)}) custom-call(s32[128]{0:T(128)} %convert_element_type.10.flag_ref, f32[1,1024]{1,0:T(1,128)} %bitcast.13, f32[2,64,1]{2,1,0:T(8,128)} %copy.12.w_ref, f32[2,64,1024]{2,1,0:T(8,128)} %bitcast.11, bf16[1024,1024]{1,0:T(8,128)(2,1)} %a_ref.3, bf16[1024,1024]{1,0:T(8,128)(2,1)} %g_ref.1), custom_call_target="tpu_custom_call" | custom-call | tf_op jit(solution)/shard_map/pallas_call | solution.py:174
  84.8 1.3 %constant_dynamic-slice_fusion.1 = f32[4,64]{1,0:T(4,128)} fusion(f32[4,1024]{1,0:T(4,128)} %get-tuple-element.18, s32[]{:T(128)S(6)} %select_n.27), kind=kLoop, calls=%fused_computation.20 | loop fusion | bytes 2052 | tf_op jit(solution)/shard_map/dynamic_slice | solution.py:294
  86.1 0.0 all-gather.2.cloned.1.call-done.s_ref
  86.1 28.0 %shard_map.79 = (f32[64,1024]{1,0:T(8,128)}, f32[64,1024]{1,0:T(8,128)}, f32[4,1024]{1,0:T(4,128)}) custom-call(f32[64,1024]{1,0:T(8,128)} %get-tuple-element.19.even_ref, f32[64,1024]{1,0:T(8,128)} %get-tuple-element.20.odd_ref, bf16[1024,1024]{1,0:T(8,128)(2,1)} %a_ref.3, bf16[1024,1024]{1,0:T(8,128)(2,1)} %all-gather.2.cloned.1.call-done.s_ref), custom_call_target="tpu_custom_call" | custom-call | tf_op jit(solution)/shard_map/pallas_call | solution.py:182
  114.1 1.3 %constant_dynamic-slice_fusion = f32[4,64]{1,0:T(4,128)} fusion(f32[4,1024]{1,0:T(4,128)} %get-tuple-element.21, s32[]{:T(128)S(6)} %select_n.27), kind=kLoop, calls=%fused_computation.19 | loop fusion | bytes 2052 | tf_op jit(solution)/shard_map/dynamic_slice | solution.py:294
  (4 shorter events, 0.1 us)
Async XLA Ops:
  7.2 78.9 %all-gather.2.cloned.1.call-start = ((), (), s32[]{:S(2)}) async-start(), calls=%async_computation | async-start | bytes 2228224 | tf_op jit(solution)/shard_map/all_gather | solution.py:289
Sparse Core Ops, SparseCore 0:
  10.1 49.0 all-gather.1

commit v11 on v10

--- a/solution.py
+++ b/solution.py
@@ -73,10 +73,19 @@
 
 def own_rows(even_ref, odd_ref, out_ref):
     per = out_ref.shape[0] // 2
+    panel = out_ref.shape[1]
+    width = even_ref.shape[1]
     base = lax.axis_index("tm") * per
+    lane = lax.axis_index("state")
+    rows = []
     for i in range(per):
-        out_ref[2 * i : 2 * i + 1, :] = even_ref[pl.ds(base + i, 1), :]
-        out_ref[2 * i + 1 : 2 * i + 2, :] = odd_ref[pl.ds(base + i, 1), :]
+        rows.append(even_ref[pl.ds(base + i, 1), :])
+        rows.append(odd_ref[pl.ds(base + i, 1), :])
+    block = jnp.concatenate(rows, axis=0)
+    picked = block[:, 0:panel]
+    for j in range(1, width // panel):
+        picked = jnp.where(lane == j, block[:, j * panel : (j + 1) * panel], picked)
+    out_ref[...] = picked
 
 
 def filter_kernel(
@@ -170,7 +179,7 @@
     square = pltpu.VMEM((width, width), F32)
     stacked = pltpu.VMEM((2, width, width), F32)
     seg = steps // lax.axis_size("tm")
-    own = jax.ShapeDtypeStruct((seg, width), F32)
+    own = jax.ShapeDtypeStruct((seg, width // lax.axis_size("state")), F32)
     f_even, f_odd, f_own = pl.pallas_call(
         filter_kernel,
         out_shape=(rows, rows, own),
@@ -290,9 +299,7 @@
     f_own, s_own = run_chain(
         weights, prior[None, :], transition, gain, smoother_full, all_observed
     )
-    c0 = lax.axis_index("state") * panel
-    block_of = lambda rows: lax.dynamic_slice_in_dim(rows, c0, panel, 1)
-    return block_of(f_own), block_of(s_own)
+    return f_own, s_own
 
 
 def solution(mesh):

time: 123 us -> 122 us (level)
  local copies, waits for them, and re-layouts: 8.23 us -> 5.58 us
  Pallas kernels: 97.8 us -> 99.7 us
    dynamic_slice x2 -> x0, local copies, waits for them, and re-layouts: 2.65 us -> none  [local(): block_of = lambda rows: lax.dynamic_slice_in_dim(rows, c0, panel, 1)]
  transfers between devices with their start and end apart: 1 -> 1, of which waited for: 0 -> 0; matrix products, arithmetic and copies ran while one was open for 7% -> 6% of each run, Pallas kernels for 57% -> 58%
where the time goes in v11:
time: 122 us
  Pallas kernels  99.7 us (82%)
  between operations  14.1 us (12%)
  local copies, waits for them, and re-layouts  5.58 us (5%)
  other arithmetic  1.46 us (1%)
    pallas_call x1, Pallas kernels, run_chain(): pl.pallas_call(filter_kernel, out_shape=(rows, rows, own), in_specs=[smem...  45.3 us
    pallas_call x1, Pallas kernels, run_chain(): pl.pallas_call(smooth_kernel, out_shape=(rows, rows, own), in_specs=[vmem...  29 us
    pallas_call x1, Pallas kernels, gather_over_time(): pl.pallas_call(functools.partial(gather_kernel, count), out_shape=jax.Sha...  25.5 us
  transfers between devices with their start and end apart: 1, of which 0 were waited for; matrix products, arithmetic and copies ran while one was open for 6% of the time, Pallas kernels for 58%

profile of v11, /device:TPU:1, one launch (start us, length us, event | category | flops | bytes accessed | tf_op | source)
XLA Modules:
  0.0 121.6 jit_solution(12358353124933714659)
XLA Ops:
  7.2 0.0 all-gather.2.cloned.1.call-start
  7.2 0.7 all-gather.2.cloned.1.call-update
  7.9 0.7 reshape.80
  8.6 0.7 convert_bitcast_fusion
  9.3 0.6 select_maximum_fusion.block_ref
  9.9 25.5 %shard_map.77 = f32[32,40,128]{2,1,0:T(8,128)} custom-call(f32[40,128]{1,0:T(8,128)} %select_maximum_fusion.block_ref), custom_call_target="tpu_custom_call" | custom-call | tf_op jit(solution)/shard_map/pallas_call | solution.py:270
  35.4 1.7 %gather_fusion = f32[32,40,128]{2,1,0:T(8,128)S(1)} fusion(f32[32,40,128]{2,1,0:T(8,128)} %shard_map.77, s32[1024]{0:T(1024)S(1)} %pad_clamp_fusion), kind=kCustom, calls=%fused_computation | custom fusion | bytes 1310848 | tf_op jit(solution)/shard_map/jit(_take)/gather | solution.py:295
  37.1 0.1 broadcast_select_fusion
  37.3 0.1 slice.27
  37.3 0.1 convert_reduce_fusion
  37.4 0.6 convert_element_type.10.flag_ref
  38.0 0.1 reshape_reshape_squeeze.3
  38.1 1.1 copy.12.w_ref
  39.2 0.3 reshape_reshape.3
  39.5 1.0 copy.16
  40.5 45.3 %shard_map.78 = (f32[64,1024]{1,0:T(8,128)}, f32[64,1024]{1,0:T(8,128)}, f32[4,64]{1,0:T(4,128)}) custom-call(s32[128]{0:T(128)} %convert_element_type.10.flag_ref, f32[1,1024]{1,0:T(1,128)} %bitcast.13, f32[2,64,1]{2,1,0:T(8,128)} %copy.12.w_ref, f32[2,64,1024]{2,1,0:T(8,128)} %bitcast.11, bf16[1024,1024]{1,0:T(8,128)(2,1)} %a_ref.3, bf16[1024,1024]{1,0:T(8,128)(2,1)} %g_ref.1), custom_call_target="tpu_custom_call" | custom-call | tf_op jit(solution)/shard_map/pallas_call | solution.py:183
  85.8 0.0 all-gather.2.cloned.1.call-done.s_ref
  85.8 29.0 %shard_map.79 = (f32[64,1024]{1,0:T(8,128)}, f32[64,1024]{1,0:T(8,128)}, f32[4,64]{1,0:T(4,128)}) custom-call(f32[64,1024]{1,0:T(8,128)} %get-tuple-element.19.even_ref, f32[64,1024]{1,0:T(8,128)} %get-tuple-element.20.odd_ref, bf16[1024,1024]{1,0:T(8,128)(2,1)} %a_ref.3, bf16[1024,1024]{1,0:T(8,128)(2,1)} %all-gather.2.cloned.1.call-done.s_ref), custom_call_target="tpu_custom_call" | custom-call | tf_op jit(solution)/shard_map/pallas_call | solution.py:191
  (4 shorter events, 0.1 us)
Async XLA Ops:
  7.2 78.6 %all-gather.2.cloned.1.call-start = ((), (), s32[]{:S(2)}) async-start(), calls=%async_computation | async-start | bytes 2228224 | tf_op jit(solution)/shard_map/all_gather | solution.py:298
Sparse Core Ops, SparseCore 0:
  10.1 49.0 all-gather.1

commit v12 on v11

--- a/solution.py
+++ b/solution.py
@@ -291,6 +291,7 @@
     flags = jnp.zeros((8, 128), F32).at[0, :seg].set(present.astype(F32))
     block = jnp.concatenate([observed.reshape(dense, 128), flags], axis=0)
     slots = gather_over_time(block)
+    smoother, slots = lax.optimization_barrier((smoother, slots))
     order = lax.rem(me - jnp.arange(count) + count, count)
     slots = jnp.take(slots, order, axis=0)
     all_observed = slots[:, :dense, :].reshape(-1, width)

time: 122 us -> 121 us (level)
  transfers between devices with their start and end apart: 1 -> 1, of which waited for: 0 -> 0; matrix products, arithmetic and copies ran while one was open for 6% -> 4% of each run, Pallas kernels for 58% -> 37%
where the time goes in v12:
time: 121 us
  Pallas kernels  99.7 us (82%)
  between operations  14.1 us (12%)
  local copies, waits for them, and re-layouts  5.56 us (5%)
  other arithmetic  1.46 us (1%)
    pallas_call x1, Pallas kernels, run_chain(): pl.pallas_call(filter_kernel, out_shape=(rows, rows, own), in_specs=[smem...  45.2 us
    pallas_call x1, Pallas kernels, run_chain(): pl.pallas_call(smooth_kernel, out_shape=(rows, rows, own), in_specs=[vmem...  29 us
    pallas_call x1, Pallas kernels, gather_over_time(): pl.pallas_call(functools.partial(gather_kernel, count), out_shape=jax.Sha...  25.5 us
  transfers between devices with their start and end apart: 1, of which 0 were waited for; matrix products, arithmetic and copies ran while one was open for 4% of the time, Pallas kernels for 37%

profile of v12, /device:TPU:1, one launch (start us, length us, event | category | flops | bytes accessed | tf_op | source)
XLA Modules:
  0.0 120.8 jit_solution(14989036930338884559)
XLA Ops:
  7.2 0.0 all-gather.2.cloned.1.call-start
  7.2 0.7 convert_bitcast_fusion
  7.9 0.7 reshape.80
  8.6 0.6 select_maximum_fusion.block_ref
  9.2 25.5 %shard_map.77 = f32[32,40,128]{2,1,0:T(8,128)} custom-call(f32[40,128]{1,0:T(8,128)} %select_maximum_fusion.block_ref), custom_call_target="tpu_custom_call" | custom-call | tf_op jit(solution)/shard_map/pallas_call | solution.py:270
  34.7 0.0 all-gather.2.cloned.1.call-update
  34.7 1.7 %gather_fusion = f32[32,40,128]{2,1,0:T(8,128)S(1)} fusion(f32[32,40,128]{2,1,0:T(8,128)} %shard_map.77, s32[1024]{0:T(1024)S(1)} %pad_clamp_fusion), kind=kCustom, calls=%fused_computation | custom fusion | bytes 1310848 | tf_op jit(solution)/shard_map/jit(_take)/gather | solution.py:296
  36.4 0.1 broadcast_select_fusion
  36.6 0.1 slice.27
  36.6 0.1 convert_reduce_fusion
  36.7 0.6 convert_element_type.10.flag_ref
  37.3 0.1 reshape_reshape_squeeze.3
  37.4 1.1 copy.12.w_ref
  38.6 0.3 reshape_reshape.3
  38.8 1.0 copy.16
  39.8 45.2 %shard_map.78 = (f32[64,1024]{1,0:T(8,128)}, f32[64,1024]{1,0:T(8,128)}, f32[4,64]{1,0:T(4,128)}) custom-call(s32[128]{0:T(128)} %convert_element_type.10.flag_ref, f32[1,1024]{1,0:T(1,128)} %bitcast.13, f32[2,64,1]{2,1,0:T(8,128)} %copy.12.w_ref, f32[2,64,1024]{2,1,0:T(8,128)} %bitcast.11, bf16[1024,1024]{1,0:T(8,128)(2,1)} %a_ref.3, bf16[1024,1024]{1,0:T(8,128)(2,1)} %g_ref.1), custom_call_target="tpu_custom_call" | custom-call | tf_op jit(solution)/shard_map/pallas_call | solution.py:183
  85.0 0.0 all-gather.2.cloned.1.call-done.s_ref
  85.0 29.0 %shard_map.79 = (f32[64,1024]{1,0:T(8,128)}, f32[64,1024]{1,0:T(8,128)}, f32[4,64]{1,0:T(4,128)}) custom-call(f32[64,1024]{1,0:T(8,128)} %get-tuple-element.22.even_ref, f32[64,1024]{1,0:T(8,128)} %get-tuple-element.23.odd_ref, bf16[1024,1024]{1,0:T(8,128)(2,1)} %a_ref.3, bf16[1024,1024]{1,0:T(8,128)(2,1)} %all-gather.2.cloned.1.call-done.s_ref), custom_call_target="tpu_custom_call" | custom-call | tf_op jit(solution)/shard_map/pallas_call | solution.py:191
  (4 shorter events, 0.1 us)
Async XLA Ops:
  7.2 77.9 %all-gather.2.cloned.1.call-start = ((), (), s32[]{:S(2)}) async-start(), calls=%async_computation | async-start | bytes 2228224 | tf_op jit(solution)/shard_map/all_gather | solution.py:299
Sparse Core Ops, SparseCore 0:
  34.8 43.2 all-gather.1

commit v13 on v11

--- a/solution.py
+++ b/solution.py
@@ -207,12 +207,6 @@
     half = count // 2
     share = half - 1
     mesh_id = pl.DeviceIdType.MESH
-    barrier = pltpu.get_barrier_semaphore()
-    for step in range(1, count):
-        peer = lax.rem(me + step, count)
-        pl.semaphore_signal(barrier, inc=1, device_id={"tm": peer}, device_id_type=mesh_id)
-    pl.semaphore_signal(barrier, inc=1, device_id={"state": sibling}, device_id_type=mesh_id)
-    pl.semaphore_wait(barrier, count)
 
     def fetch(step):
         peer = lax.rem(me + step, count)
@@ -278,7 +272,7 @@
             pltpu.SemaphoreType.DMA((count,)),
             pltpu.SemaphoreType.DMA((2,)),
         ],
-        compiler_params=pltpu.CompilerParams(collective_id=0, has_side_effects=True),
+        compiler_params=pltpu.CompilerParams(has_side_effects=True),
     )(block)
 
 

time: 122 us -> 134 us (1.098)
  Pallas kernels: 99.7 us -> 112 us
    pallas_call x1, Pallas kernels: 25.5 us -> 37.3 us  [gather_over_time(): pl.pallas_call(functools.partial(gather_kernel, count), out_shape=jax.Sha...]
  transfers between devices with their start and end apart: 1 -> 1, of which waited for: 0 -> 0; matrix products, arithmetic and copies ran while one was open for 6% -> 5% of each run, Pallas kernels for 58% -> 62%
where the time goes in v13:
time: 134 us; the launch traced here: 133 us
  Pallas kernels  112 us (84%)
  between operations  14.1 us (11%)
  local copies, waits for them, and re-layouts  5.57 us (4%)
  other arithmetic  1.46 us (1%)
    pallas_call x1, Pallas kernels, run_chain(): pl.pallas_call(filter_kernel, out_shape=(rows, rows, own), in_specs=[smem...  45.3 us
    pallas_call x1, Pallas kernels, gather_over_time(): pl.pallas_call(functools.partial(gather_kernel, count), out_shape=jax.Sha...  37.3 us
    pallas_call x1, Pallas kernels, run_chain(): pl.pallas_call(smooth_kernel, out_shape=(rows, rows, own), in_specs=[vmem...  29 us
  transfers between devices with their start and end apart: 1, of which 0 were waited for; matrix products, arithmetic and copies ran while one was open for 5% of the time, Pallas kernels for 62%

profile of v13, /device:TPU:1, one launch (start us, length us, event | category | flops | bytes accessed | tf_op | source)
XLA Modules:
  0.0 133.4 jit_solution(9839132462873626493)
XLA Ops:
  7.2 0.0 all-gather.2.cloned.1.call-start
  7.2 0.7 all-gather.2.cloned.1.call-update
  7.9 0.7 reshape.80
  8.6 0.7 convert_bitcast_fusion
  9.3 0.6 select_maximum_fusion.block_ref
  9.9 37.3 %shard_map.77 = f32[32,40,128]{2,1,0:T(8,128)} custom-call(f32[40,128]{1,0:T(8,128)} %select_maximum_fusion.block_ref), custom_call_target="tpu_custom_call" | custom-call | tf_op jit(solution)/shard_map/pallas_call | solution.py:264
  47.3 1.7 %gather_fusion = f32[32,40,128]{2,1,0:T(8,128)S(1)} fusion(f32[32,40,128]{2,1,0:T(8,128)} %shard_map.77, s32[1024]{0:T(1024)S(1)} %pad_clamp_fusion), kind=kCustom, calls=%fused_computation | custom fusion | bytes 1310848 | tf_op jit(solution)/shard_map/jit(_take)/gather | solution.py:289
  49.0 0.1 broadcast_select_fusion
  49.1 0.1 slice.27
  49.2 0.1 convert_reduce_fusion
  49.2 0.6 convert_element_type.10.flag_ref
  49.9 0.1 reshape_reshape_squeeze.3
  49.9 1.1 copy.12.w_ref
  51.1 0.3 reshape_reshape.3
  51.4 1.0 copy.16
  52.3 45.3 %shard_map.78 = (f32[64,1024]{1,0:T(8,128)}, f32[64,1024]{1,0:T(8,128)}, f32[4,64]{1,0:T(4,128)}) custom-call(s32[128]{0:T(128)} %convert_element_type.10.flag_ref, f32[1,1024]{1,0:T(1,128)} %bitcast.13, f32[2,64,1]{2,1,0:T(8,128)} %copy.12.w_ref, f32[2,64,1024]{2,1,0:T(8,128)} %bitcast.11, bf16[1024,1024]{1,0:T(8,128)(2,1)} %a_ref.3, bf16[1024,1024]{1,0:T(8,128)(2,1)} %g_ref.1), custom_call_target="tpu_custom_call" | custom-call | tf_op jit(solution)/shard_map/pallas_call | solution.py:183
  97.6 0.0 all-gather.2.cloned.1.call-done.s_ref
  97.6 29.0 %shard_map.79 = (f32[64,1024]{1,0:T(8,128)}, f32[64,1024]{1,0:T(8,128)}, f32[4,64]{1,0:T(4,128)}) custom-call(f32[64,1024]{1,0:T(8,128)} %get-tuple-element.19.even_ref, f32[64,1024]{1,0:T(8,128)} %get-tuple-element.20.odd_ref, bf16[1024,1024]{1,0:T(8,128)(2,1)} %a_ref.3, bf16[1024,1024]{1,0:T(8,128)(2,1)} %all-gather.2.cloned.1.call-done.s_ref), custom_call_target="tpu_custom_call" | custom-call | tf_op jit(solution)/shard_map/pallas_call | solution.py:191
  (4 shorter events, 0.1 us)
Async XLA Ops:
  7.2 90.4 %all-gather.2.cloned.1.call-start = ((), (), s32[]{:S(2)}) async-start(), calls=%async_computation | async-start | bytes 2228224 | tf_op jit(solution)/shard_map/all_gather | solution.py:292
Sparse Core Ops, SparseCore 0:
  10.1 49.2 all-gather.1

commit v14 on v12

--- a/solution.py
+++ b/solution.py
@@ -208,11 +208,20 @@
     share = half - 1
     mesh_id = pl.DeviceIdType.MESH
     barrier = pltpu.get_barrier_semaphore()
-    for step in range(1, count):
-        peer = lax.rem(me + step, count)
+
+    def greet(step):
+        peer = lax.rem(me - step + count, count)
         pl.semaphore_signal(barrier, inc=1, device_id={"tm": peer}, device_id_type=mesh_id)
+
+    for j in range(half - 1):
+        greet(core * (half - 1) + j + 1)
+
+    @pl.when(core == 1)
+    def _():
+        greet(count - 1)
+
     pl.semaphore_signal(barrier, inc=1, device_id={"state": sibling}, device_id_type=mesh_id)
-    pl.semaphore_wait(barrier, count)
+    pl.semaphore_wait(barrier, half + core)
 
     def fetch(step):
         peer = lax.rem(me + step, count)

time: 121 us -> 122 us (level)
  no operation moved by 1% of the time
where the time goes in v14:
time: 122 us
  Pallas kernels  100 us (82%)
  between operations  14.1 us (12%)
  local copies, waits for them, and re-layouts  5.56 us (5%)
  other arithmetic  1.46 us (1%)
    pallas_call x1, Pallas kernels, run_chain(): pl.pallas_call(filter_kernel, out_shape=(rows, rows, own), in_specs=[smem...  45.2 us
    pallas_call x1, Pallas kernels, run_chain(): pl.pallas_call(smooth_kernel, out_shape=(rows, rows, own), in_specs=[vmem...  29 us
    pallas_call x1, Pallas kernels, gather_over_time(): pl.pallas_call(functools.partial(gather_kernel, count), out_shape=jax.Sha...  26.3 us
  transfers between devices with their start and end apart: 1, of which 0 were waited for; matrix products, arithmetic and copies ran while one was open for 4% of the time, Pallas kernels for 37%

profile of v14, /device:TPU:1, one launch (start us, length us, event | category | flops | bytes accessed | tf_op | source)
XLA Modules:
  0.0 121.7 jit_solution(9880539747450897281)
XLA Ops:
  7.2 0.0 all-gather.2.cloned.1.call-start
  7.2 0.7 convert_bitcast_fusion
  7.9 0.7 reshape.80
  8.6 0.6 select_maximum_fusion.block_ref
  9.2 26.3 %shard_map.77 = f32[32,40,128]{2,1,0:T(8,128)} custom-call(f32[40,128]{1,0:T(8,128)} %select_maximum_fusion.block_ref), custom_call_target="tpu_custom_call" | custom-call | tf_op jit(solution)/shard_map/pallas_call | solution.py:279
  35.5 0.0 all-gather.2.cloned.1.call-update
  35.5 1.7 %gather_fusion = f32[32,40,128]{2,1,0:T(8,128)S(1)} fusion(f32[32,40,128]{2,1,0:T(8,128)} %shard_map.77, s32[1024]{0:T(1024)S(1)} %pad_clamp_fusion), kind=kCustom, calls=%fused_computation | custom fusion | bytes 1310848 | tf_op jit(solution)/shard_map/jit(_take)/gather | solution.py:305
  37.2 0.1 broadcast_select_fusion
  37.4 0.1 slice.27
  37.4 0.1 convert_reduce_fusion
  37.5 0.6 convert_element_type.10.flag_ref
  38.2 0.1 reshape_reshape_squeeze.3
  38.2 1.1 copy.12.w_ref
  39.4 0.3 reshape_reshape.3
  39.6 1.0 copy.16
  40.6 45.2 %shard_map.78 = (f32[64,1024]{1,0:T(8,128)}, f32[64,1024]{1,0:T(8,128)}, f32[4,64]{1,0:T(4,128)}) custom-call(s32[128]{0:T(128)} %convert_element_type.10.flag_ref, f32[1,1024]{1,0:T(1,128)} %bitcast.13, f32[2,64,1]{2,1,0:T(8,128)} %copy.12.w_ref, f32[2,64,1024]{2,1,0:T(8,128)} %bitcast.11, bf16[1024,1024]{1,0:T(8,128)(2,1)} %a_ref.3, bf16[1024,1024]{1,0:T(8,128)(2,1)} %g_ref.1), custom_call_target="tpu_custom_call" | custom-call | tf_op jit(solution)/shard_map/pallas_call | solution.py:183
  85.8 0.0 all-gather.2.cloned.1.call-done.s_ref
  85.8 29.0 %shard_map.79 = (f32[64,1024]{1,0:T(8,128)}, f32[64,1024]{1,0:T(8,128)}, f32[4,64]{1,0:T(4,128)}) custom-call(f32[64,1024]{1,0:T(8,128)} %get-tuple-element.22.even_ref, f32[64,1024]{1,0:T(8,128)} %get-tuple-element.23.odd_ref, bf16[1024,1024]{1,0:T(8,128)(2,1)} %a_ref.3, bf16[1024,1024]{1,0:T(8,128)(2,1)} %all-gather.2.cloned.1.call-done.s_ref), custom_call_target="tpu_custom_call" | custom-call | tf_op jit(solution)/shard_map/pallas_call | solution.py:191
  (4 shorter events, 0.1 us)
Async XLA Ops:
  7.2 78.7 %all-gather.2.cloned.1.call-start = ((), (), s32[]{:S(2)}) async-start(), calls=%async_computation | async-start | bytes 2228224 | tf_op jit(solution)/shard_map/all_gather | solution.py:308
Sparse Core Ops, SparseCore 0:
  35.6 42.5 all-gather.1

commit v15 on v12

--- a/solution.py
+++ b/solution.py
@@ -111,7 +111,7 @@
         odd_ref[pl.ds(i, 1), :] = updated
         return updated
 
-    lax.fori_loop(0, half, pair_step, prior_ref[...])
+    lax.fori_loop(0, half, pair_step, prior_ref[...], unroll=2)
     prev_ref[0:1, :] = prior_ref[...]
     prev_ref[1:half, :] = odd_ref[0 : half - 1, :]
     predicted = times_transpose(prev_ref[...], transition)
@@ -151,7 +151,7 @@
         s_odd_ref[pl.ds(q - 2, 1), :] = value
         return value
 
-    lax.fori_loop(0, half // 2 - 1, quad_step, last)
+    lax.fori_loop(0, half // 2 - 1, quad_step, last, unroll=2)
     odd_row = lax.broadcasted_iota(jnp.int32, (half, 1), 0) % 2 == 1
     first = times_transpose(s_odd_ref[...], smoother) + d_even
     s_even_ref[...] = jnp.where(odd_row, first, 0.0)

time: 121 us -> 121 us (level)
  no operation moved by 1% of the time
where the time goes in v15:
time: 121 us; the launch traced here: 120 us
  Pallas kernels  99.2 us (82%)
  between operations  14.1 us (12%)
  local copies, waits for them, and re-layouts  5.56 us (5%)
  other arithmetic  1.46 us (1%)
    pallas_call x1, Pallas kernels, run_chain(): pl.pallas_call(filter_kernel, out_shape=(rows, rows, own), in_specs=[smem...  44.9 us
    pallas_call x1, Pallas kernels, run_chain(): pl.pallas_call(smooth_kernel, out_shape=(rows, rows, own), in_specs=[vmem...  28.8 us
    pallas_call x1, Pallas kernels, gather_over_time(): pl.pallas_call(functools.partial(gather_kernel, count), out_shape=jax.Sha...  25.5 us
  transfers between devices with their start and end apart: 1, of which 0 were waited for; matrix products, arithmetic and copies ran while one was open for 4% of the time, Pallas kernels for 37%

profile of v15, /device:TPU:1, one launch (start us, length us, event | category | flops | bytes accessed | tf_op | source)
XLA Modules:
  0.0 120.4 jit_solution(5128567395534459296)
XLA Ops:
  7.2 0.0 all-gather.2.cloned.1.call-start
  7.2 0.7 convert_bitcast_fusion
  7.9 0.7 reshape.80
  8.6 0.6 select_maximum_fusion.block_ref
  9.2 25.5 %shard_map.77 = f32[32,40,128]{2,1,0:T(8,128)} custom-call(f32[40,128]{1,0:T(8,128)} %select_maximum_fusion.block_ref), custom_call_target="tpu_custom_call" | custom-call | tf_op jit(solution)/shard_map/pallas_call | solution.py:270
  34.7 0.0 all-gather.2.cloned.1.call-update
  34.7 1.7 %gather_fusion = f32[32,40,128]{2,1,0:T(8,128)S(1)} fusion(f32[32,40,128]{2,1,0:T(8,128)} %shard_map.77, s32[1024]{0:T(1024)S(1)} %pad_clamp_fusion), kind=kCustom, calls=%fused_computation | custom fusion | bytes 1310848 | tf_op jit(solution)/shard_map/jit(_take)/gather | solution.py:296
  36.4 0.1 broadcast_select_fusion
  36.6 0.1 slice.27
  36.6 0.1 convert_reduce_fusion
  36.7 0.6 convert_element_type.10.flag_ref
  37.3 0.1 reshape_reshape_squeeze.3
  37.4 1.1 copy.12.w_ref
  38.6 0.3 reshape_reshape.3
  38.8 1.0 copy.16
  39.8 44.9 %shard_map.78 = (f32[64,1024]{1,0:T(8,128)}, f32[64,1024]{1,0:T(8,128)}, f32[4,64]{1,0:T(4,128)}) custom-call(s32[128]{0:T(128)} %convert_element_type.10.flag_ref, f32[1,1024]{1,0:T(1,128)} %bitcast.13, f32[2,64,1]{2,1,0:T(8,128)} %copy.12.w_ref, f32[2,64,1024]{2,1,0:T(8,128)} %bitcast.11, bf16[1024,1024]{1,0:T(8,128)(2,1)} %a_ref.3, bf16[1024,1024]{1,0:T(8,128)(2,1)} %g_ref.1), custom_call_target="tpu_custom_call" | custom-call | tf_op jit(solution)/shard_map/pallas_call | solution.py:183
  84.7 0.0 all-gather.2.cloned.1.call-done.s_ref
  84.7 28.8 %shard_map.79 = (f32[64,1024]{1,0:T(8,128)}, f32[64,1024]{1,0:T(8,128)}, f32[4,64]{1,0:T(4,128)}) custom-call(f32[64,1024]{1,0:T(8,128)} %get-tuple-element.22.even_ref, f32[64,1024]{1,0:T(8,128)} %get-tuple-element.23.odd_ref, bf16[1024,1024]{1,0:T(8,128)(2,1)} %a_ref.3, bf16[1024,1024]{1,0:T(8,128)(2,1)} %all-gather.2.cloned.1.call-done.s_ref), custom_call_target="tpu_custom_call" | custom-call | tf_op jit(solution)/shard_map/pallas_call | solution.py:191
  (4 shorter events, 0.1 us)
Async XLA Ops:
  7.2 77.5 %all-gather.2.cloned.1.call-start = ((), (), s32[]{:S(2)}) async-start(), calls=%async_computation | async-start | bytes 2228224 | tf_op jit(solution)/shard_map/all_gather | solution.py:299
Sparse Core Ops, SparseCore 0:
  34.8 43.2 all-gather.1

commit v16 on v15

--- a/solution.py
+++ b/solution.py
@@ -111,7 +111,7 @@
         odd_ref[pl.ds(i, 1), :] = updated
         return updated
 
-    lax.fori_loop(0, half, pair_step, prior_ref[...], unroll=2)
+    lax.fori_loop(0, half, pair_step, prior_ref[...], unroll=4)
     prev_ref[0:1, :] = prior_ref[...]
     prev_ref[1:half, :] = odd_ref[0 : half - 1, :]
     predicted = times_transpose(prev_ref[...], transition)

time: 121 us -> 120 us (level)
  no operation moved by 1% of the time
where the time goes in v16:
time: 120 us
  Pallas kernels  99 us (82%)
  between operations  14.1 us (12%)
  local copies, waits for them, and re-layouts  5.56 us (5%)
  other arithmetic  1.46 us (1%)
    pallas_call x1, Pallas kernels, run_chain(): pl.pallas_call(filter_kernel, out_shape=(rows, rows, own), in_specs=[smem...  44.7 us
    pallas_call x1, Pallas kernels, run_chain(): pl.pallas_call(smooth_kernel, out_shape=(rows, rows, own), in_specs=[vmem...  28.8 us
    pallas_call x1, Pallas kernels, gather_over_time(): pl.pallas_call(functools.partial(gather_kernel, count), out_shape=jax.Sha...  25.5 us
  transfers between devices with their start and end apart: 1, of which 0 were waited for; matrix products, arithmetic and copies ran while one was open for 4% of the time, Pallas kernels for 37%

profile of v16, /device:TPU:1, one launch (start us, length us, event | category | flops | bytes accessed | tf_op | source)
XLA Modules:
  0.0 120.2 jit_solution(7497090754880902258)
XLA Ops:
  7.2 0.0 all-gather.2.cloned.1.call-start
  7.2 0.7 convert_bitcast_fusion
  7.9 0.7 reshape.80
  8.6 0.6 select_maximum_fusion.block_ref
  9.2 25.5 %shard_map.77 = f32[32,40,128]{2,1,0:T(8,128)} custom-call(f32[40,128]{1,0:T(8,128)} %select_maximum_fusion.block_ref), custom_call_target="tpu_custom_call" | custom-call | tf_op jit(solution)/shard_map/pallas_call | solution.py:270
  34.7 0.0 all-gather.2.cloned.1.call-update
  34.7 1.7 %gather_fusion = f32[32,40,128]{2,1,0:T(8,128)S(1)} fusion(f32[32,40,128]{2,1,0:T(8,128)} %shard_map.77, s32[1024]{0:T(1024)S(1)} %pad_clamp_fusion), kind=kCustom, calls=%fused_computation | custom fusion | bytes 1310848 | tf_op jit(solution)/shard_map/jit(_take)/gather | solution.py:296
  36.4 0.1 broadcast_select_fusion
  36.6 0.1 slice.27
  36.6 0.1 convert_reduce_fusion
  36.7 0.6 convert_element_type.10.flag_ref
  37.3 0.1 reshape_reshape_squeeze.3
  37.4 1.1 copy.12.w_ref
  38.6 0.3 reshape_reshape.3
  38.8 1.0 copy.16
  39.8 44.7 %shard_map.78 = (f32[64,1024]{1,0:T(8,128)}, f32[64,1024]{1,0:T(8,128)}, f32[4,64]{1,0:T(4,128)}) custom-call(s32[128]{0:T(128)} %convert_element_type.10.flag_ref, f32[1,1024]{1,0:T(1,128)} %bitcast.13, f32[2,64,1]{2,1,0:T(8,128)} %copy.12.w_ref, f32[2,64,1024]{2,1,0:T(8,128)} %bitcast.11, bf16[1024,1024]{1,0:T(8,128)(2,1)} %a_ref.3, bf16[1024,1024]{1,0:T(8,128)(2,1)} %g_ref.1), custom_call_target="tpu_custom_call" | custom-call | tf_op jit(solution)/shard_map/pallas_call | solution.py:183
  84.5 0.0 all-gather.2.cloned.1.call-done.s_ref
  84.5 28.8 %shard_map.79 = (f32[64,1024]{1,0:T(8,128)}, f32[64,1024]{1,0:T(8,128)}, f32[4,64]{1,0:T(4,128)}) custom-call(f32[64,1024]{1,0:T(8,128)} %get-tuple-element.22.even_ref, f32[64,1024]{1,0:T(8,128)} %get-tuple-element.23.odd_ref, bf16[1024,1024]{1,0:T(8,128)(2,1)} %a_ref.3, bf16[1024,1024]{1,0:T(8,128)(2,1)} %all-gather.2.cloned.1.call-done.s_ref), custom_call_target="tpu_custom_call" | custom-call | tf_op jit(solution)/shard_map/pallas_call | solution.py:191
  (4 shorter events, 0.1 us)
Async XLA Ops:
  7.2 77.4 %all-gather.2.cloned.1.call-start = ((), (), s32[]{:S(2)}) async-start(), calls=%async_computation | async-start | bytes 2228224 | tf_op jit(solution)/shard_map/all_gather | solution.py:299
Sparse Core Ops, SparseCore 0:
  34.8 43.2 all-gather.1

commit v17 on v15

--- a/solution.py
+++ b/solution.py
@@ -105,8 +105,8 @@
     extra_ref[...] = moved - w_odd * times_transpose(moved, gain) + corr_odd
 
     def pair_step(i, state):
-        middle = column_from_row(pair_ref[flag_ref[2 * i]], state)
-        updated = row_from_column(pair_t_ref[flag_ref[2 * i + 1]], middle)
+        middle = column_from_row(pair_ref[flag_ref[2 * i].astype(jnp.int32)], state)
+        updated = row_from_column(pair_t_ref[flag_ref[2 * i + 1].astype(jnp.int32)], middle)
         updated = updated + extra_ref[pl.ds(i, 1), :]
         odd_ref[pl.ds(i, 1), :] = updated
         return updated
@@ -172,7 +172,7 @@
     vmem = pl.BlockSpec(memory_space=pltpu.VMEM)
     smem = pl.BlockSpec(memory_space=pltpu.SMEM)
     params = pltpu.CompilerParams(vmem_limit_bytes=VMEM_LIMIT)
-    flags = weights.astype(jnp.int32)
+    flags = weights
     w_pair = weights.reshape(half, 2).T[:, :, None]
     y_pair = observed.reshape(half, 2, width).transpose(1, 0, 2)
     rows = jax.ShapeDtypeStruct((half, width), F32)

time: 121 us -> 121 us (level)
  no operation moved by 1% of the time
where the time goes in v17:
time: 121 us; the launch traced here: 120 us
  Pallas kernels  99.3 us (82%)
  between operations  14.1 us (12%)
  local copies, waits for them, and re-layouts  5.56 us (5%)
  other arithmetic  1.41 us (1%)
    pallas_call x1, Pallas kernels, run_chain(): pl.pallas_call(filter_kernel, out_shape=(rows, rows, own), in_specs=[smem...  45 us
    pallas_call x1, Pallas kernels, run_chain(): pl.pallas_call(smooth_kernel, out_shape=(rows, rows, own), in_specs=[vmem...  28.8 us
    pallas_call x1, Pallas kernels, gather_over_time(): pl.pallas_call(functools.partial(gather_kernel, count), out_shape=jax.Sha...  25.5 us
  transfers between devices with their start and end apart: 1, of which 0 were waited for; matrix products, arithmetic and copies ran while one was open for 4% of the time, Pallas kernels for 37%

profile of v17, /device:TPU:1, one launch (start us, length us, event | category | flops | bytes accessed | tf_op | source)
XLA Modules:
  0.0 120.4 jit_solution(16365017793873517551)
XLA Ops:
  7.2 0.0 all-gather.2.cloned.1.call-start
  7.2 0.7 convert_bitcast_fusion
  7.9 0.7 reshape.79
  8.6 0.6 select_maximum_fusion.block_ref
  9.2 25.5 %shard_map.77 = f32[32,40,128]{2,1,0:T(8,128)} custom-call(f32[40,128]{1,0:T(8,128)} %select_maximum_fusion.block_ref), custom_call_target="tpu_custom_call" | custom-call | tf_op jit(solution)/shard_map/pallas_call | solution.py:270
  34.7 0.0 all-gather.2.cloned.1.call-update
  34.7 1.7 %gather_fusion = f32[32,40,128]{2,1,0:T(8,128)S(1)} fusion(f32[32,40,128]{2,1,0:T(8,128)} %shard_map.77, s32[1024]{0:T(1024)S(1)} %pad_clamp_fusion), kind=kCustom, calls=%fused_computation | custom fusion | bytes 1310848 | tf_op jit(solution)/shard_map/jit(_take)/gather | solution.py:296
  36.5 0.1 broadcast_select_fusion
  36.6 0.1 slice.27
  36.7 0.6 reshape_squeeze.3.flag_ref
  37.3 0.1 reshape_reshape_squeeze.3
  37.4 1.1 copy.12.w_ref
  38.5 0.3 reshape_reshape.3
  38.8 1.0 copy.16
  39.7 45.0 %shard_map.78 = (f32[64,1024]{1,0:T(8,128)}, f32[64,1024]{1,0:T(8,128)}, f32[4,64]{1,0:T(4,128)}) custom-call(f32[128]{0:T(128)} %reshape_squeeze.3.flag_ref, f32[1,1024]{1,0:T(1,128)} %bitcast.15, f32[2,64,1]{2,1,0:T(8,128)} %copy.12.w_ref, f32[2,64,1024]{2,1,0:T(8,128)} %bitcast.12, bf16[1024,1024]{1,0:T(8,128)(2,1)} %a_ref.3, bf16[1024,1024]{1,0:T(8,128)(2,1)} %g_ref.1), custom_call_target="tpu_custom_call" | custom-call | tf_op jit(solution)/shard_map/pallas_call | solution.py:183
  84.7 0.0 all-gather.2.cloned.1.call-done.s_ref
  84.7 28.8 %shard_map.79 = (f32[64,1024]{1,0:T(8,128)}, f32[64,1024]{1,0:T(8,128)}, f32[4,64]{1,0:T(4,128)}) custom-call(f32[64,1024]{1,0:T(8,128)} %get-tuple-element.22.even_ref, f32[64,1024]{1,0:T(8,128)} %get-tuple-element.23.odd_ref, bf16[1024,1024]{1,0:T(8,128)(2,1)} %a_ref.3, bf16[1024,1024]{1,0:T(8,128)(2,1)} %all-gather.2.cloned.1.call-done.s_ref), custom_call_target="tpu_custom_call" | custom-call | tf_op jit(solution)/shard_map/pallas_call | solution.py:191
  (4 shorter events, 0.1 us)
Async XLA Ops:
  7.2 77.6 %all-gather.2.cloned.1.call-start = ((), (), s32[]{:S(2)}) async-start(), calls=%async_computation | async-start | bytes 2228224 | tf_op jit(solution)/shard_map/all_gather | solution.py:299
Sparse Core Ops, SparseCore 0:
  34.8 43.1 all-gather.1
